TPU v7x, 32 devices: a whole 2x2x4 slice. The times are simulated.
32 devices in a mesh: group: 2 (over y), tensor: 4 (over z), dp: 4 (over x, core).
Axes of the slice: x: 2, y: 2, z: 4, core: 2. Of those that a mesh axis runs over, the one named last changes fastest.
Arguments:
- tokens: bfloat16 [2048, 4096], P(('group', 'dp'), 'tensor'), parts along dimension 0, may hold values from -6 to 6
- gate_weight: bfloat16 [4096, 15360], P('dp', 'tensor'), may hold values from -0.09375 to 0.09375
- up_weight: bfloat16 [4096, 15360], P('dp', 'tensor'), may hold values from -0.09375 to 0.09375
- grad_hidden: bfloat16 [2048, 15360], P(('group', 'dp'), 'tensor'), parts along dimension 0, may hold values from -6 to 6
- chosen_mask: int32 [2048], P(('group', 'dp')), parts along dimension 0, may hold values 0 or 1
- rejected_mask: int32 [2048], P(('group', 'dp')), parts along dimension 0, may hold values 0 or 1
- margins: float32 [32], P(('group', 'dp')), parts along dimension 0, may hold values from -6 to 6
Outputs:
- hidden: bfloat16 [2048, 15360], P(('group', 'dp'), 'tensor'), parts along dimension 0
- grad_tokens: bfloat16 [2048, 4096], P(('group', 'dp'), 'tensor'), parts along dimension 0
- grad_gate_weight: bfloat16 [8192, 15360], P(('group', 'dp'), 'tensor'), parts along dimension 0
- grad_up_weight: bfloat16 [8192, 15360], P(('group', 'dp'), 'tensor'), parts along dimension 0
There are 2 independent parts, one for each index of `group`. A program takes and returns all parts, laid end to end along the dimension named above; an argument that names none is the same for every part. Nothing has to cross between parts.
All inputs are finite; a program needn't handle non-finite values. No bound on the sum of `chosen_mask` or of `rejected_mask` on one device may be relied on, other than what follows from the above.
Results may differ from a plain program's by a relative error of at most 0.012.
Values may be sent and summed in bfloat16 or wider, within the bound.
No kernel may reach another device: no remote copies, remote signals or barrier semaphores. Data moves between devices by JAX's collectives and lax.ppermute only.
A program may use at most 384 MiB of HBM per device.

v0:
```python
import jax
import jax.numpy as jnp
from jax import lax
from jax.experimental import pallas as pl
from jax.experimental.pallas import tpu as pltpu
from jax.sharding import PartitionSpec as P

PAIR_LEN = 64
dpo_beta = 0.5
CORES = 2
SIXTEENTHS = (2, 5, 4, 5)
LAST_SPLIT = (5,)
FINAL = ((0, 4), (4, 1))
BLOCK = 768
SHORT = 4
bf16 = jnp.bfloat16
f32 = jnp.float32
ANY = pl.BlockSpec(memory_space=pl.ANY)
SMEM = pl.BlockSpec(memory_space=pltpu.SMEM)
VMEM = pl.BlockSpec(memory_space=pltpu.VMEM)


def token_route(n_tensor, n_dp):
    n_x = n_dp // CORES
    run = n_tensor // n_x
    pairs = []
    for t in range(n_tensor):
        for d in range(n_dp):
            x_src, c = divmod(d, CORES)
            x_dst, f = divmod(t, run)
            f_rel = (f - c * (run // CORES)) % run
            x_rel = (x_src - x_dst) % n_x
            pairs.append((t * n_dp + d, (x_rel * run + f_rel) * n_dp + x_dst * CORES + c))
    return pairs


def dot(a, b):
    return jnp.dot(a, b, preferred_element_type=f32)


def dot_nt(a, b):
    return lax.dot_general(a, b, (((1,), (1,)), ((), ())), preferred_element_type=f32)


def call(body, grid, ins, outs, deps=(), scratch=(), aliases=None, mib=48, flops=1, nbytes=1):
    n_in, n_dep = len(ins), len(deps)

    def wrapped(*refs):
        body(*refs[:n_in], *refs[n_in + n_dep:])

    return pl.pallas_call(
        wrapped,
        grid=grid,
        in_specs=[spec for _, spec in ins] + [ANY] * n_dep,
        out_specs=[spec for _, _, spec in outs],
        out_shape=[jax.ShapeDtypeStruct(shape, dtype) for shape, dtype, _ in outs],
        scratch_shapes=list(scratch),
        input_output_aliases=aliases or {},
        compiler_params=pltpu.CompilerParams(
            dimension_semantics=("arbitrary",) * len(grid), vmem_limit_bytes=mib << 20),
        cost_estimate=pl.CostEstimate(flops=flops, transcendentals=0, bytes_accessed=nbytes),
    )(*[a for a, _ in ins], *deps)


def forward_tile(near, far, weights, deps, n_x, block):
    rows = near.shape[0] // n_x
    feat, width = weights[0][0].shape
    n = len(weights)

    def body(near_ref, far_ref, *refs):
        own_ref, send_ref = refs[2 * n:]
        for m in range(n):
            part = dot(near_ref[...], refs[2 * m][...]) + dot(far_ref[...], refs[2 * m + 1][...])
            own_ref[m] = part[:rows]
            for s in range(1, n_x):
                send_ref[s - 1, m] = part[s * rows:(s + 1) * rows].astype(bf16)

    w_spec = pl.BlockSpec((feat, block), lambda i: (0, i))
    full = pl.BlockSpec(near.shape, lambda i: (0, 0))
    return call(
        body, (width // block,),
        [(near, full), (far, full)] + [(w, w_spec) for pair in weights for w in pair],
        [((n, rows, width), f32, pl.BlockSpec((n, rows, block), lambda i: (0, 0, i))),
         ((n_x - 1, n, rows, width), bf16, pl.BlockSpec((n_x - 1, n, rows, block), lambda i: (0, 0, 0, i)))],
        deps, flops=4 * n * n_x * rows * feat * width, nbytes=4 * n * feat * width)


def gate_tile(gate_terms, up_terms, grad_hidden, token_weight, deps, block, row_start, start, count):
    rows = token_weight.shape[0]
    n = len(gate_terms)

    def body(*refs):
        gh_ref, tw_ref, hidden_ref, mine_ref = refs[2 * n:]
        gate, up = refs[0][0], refs[n][0]
        for k in range(1, n):
            gate = gate + refs[k][0].astype(f32)
            up = up + refs[n + k][0].astype(f32)
        sig = 1.0 / (1.0 + jnp.exp(-gate))
        hidden_ref[...] = (gate * sig * up).astype(bf16)
        cot = tw_ref[...] * gh_ref[...].astype(f32)
        mine_ref[0] = (cot * up * sig * (1.0 + gate * (1.0 - sig))).astype(bf16)
        mine_ref[1] = (cot * gate * sig).astype(bf16)

    if row_start % rows:
        grad_hidden = grad_hidden[row_start:row_start + rows]
        row_start = 0
    ins = [(a, pl.BlockSpec((1, rows, block), lambda i, m=m: (m, 0, start + i))) for a, m in gate_terms + up_terms]
    ins += [(grad_hidden, pl.BlockSpec((rows, block), lambda i: (row_start // rows, start + i))),
            (token_weight, pl.BlockSpec((rows, 1), lambda i: (0, 0)))]
    cols = count * block
    return call(
        body, (count,), ins,
        [((rows, cols), bf16, pl.BlockSpec((rows, block), lambda i: (0, i))),
         ((2, rows, cols), bf16, pl.BlockSpec((2, rows, block), lambda i: (0, 0, i)))],
        deps, mib=32, flops=40 * rows * cols, nbytes=20 * rows * cols)


def token_grad_tile(grads, weights, before, deps, z, n_x, n_tensor, block, start, count, final, split):
    feat = weights[0].shape[0]
    flat = [g for per_x in grads for g in per_x]
    n = len(flat)
    rows = sum(g.shape[1] for g in grads[0])
    total = rows * n_x
    wide = n_x * feat * CORES // n_tensor
    per_core = feat // wide
    split = split and final and n_tensor == SHORT

    def body(z_ref, *refs):
        g_refs = refs[:n]
        ws = refs[n:n + 4]
        rest = refs[n + 4:]
        if before is not None:
            before_ref, rest = rest[0], rest[1:]
        both_ref, *out_refs, acc_ref = rest
        i = pl.program_id(0)
        gg = jnp.concatenate([r[0] for r in g_refs], axis=0)
        gu = jnp.concatenate([r[1] for r in g_refs], axis=0)
        both_ref[0] = gg
        both_ref[1] = gu
        near = dot_nt(gg, ws[0][...]) + dot_nt(gu, ws[1][...])
        far = dot_nt(gg, ws[2][...]) + dot_nt(gu, ws[3][...])

        @pl.when(i == 0)
        def _():
            if before is None:
                acc_ref[0] = near
                acc_ref[1] = far
            else:
                acc_ref[0] = before_ref[0] + near
                acc_ref[1] = before_ref[1] + far

        @pl.when(i > 0)
        def _():
            acc_ref[0] += near
            acc_ref[1] += far

        @pl.when(i == count - 1)
        def _():
            if not final:
                out_refs[0][...] = acc_ref[...]
                return
            sums = [acc_ref[c] for c in range(CORES)]
            for x in range(n_x):
                for c in range(CORES):
                    value = sums[c][x * rows:(x + 1) * rows]
                    if not split:
                        out_refs[0][x, c] = value.astype(bf16)
                        continue
                    for k in range(per_core):
                        b = (x * CORES + c) * per_core + k
                        part = value[:, k * wide:(k + 1) * wide]
                        for s in range(n_tensor):
                            @pl.when(z_ref[0] == b ^ s)
                            def _():
                                if s < 2:
                                    out_refs[0][s] = part
                                else:
                                    out_refs[1][s - 2] = part.astype(bf16)

    w_spec = pl.BlockSpec((feat, block), lambda i: (0, start + i))
    ins = [(z, SMEM)] + [(g, pl.BlockSpec((2, g.shape[1], block), lambda i: (0, 0, i))) for g in flat]
    ins += [(w, w_spec) for w in weights]

    def fixed(shape, dtype):
        return (shape, dtype, pl.BlockSpec(shape, lambda i: (0,) * len(shape)))

    acc_shape = (CORES, total, feat)
    if before is not None:
        ins.append((before, fixed(acc_shape, f32)[2]))
    cols = count * block
    outs = [((2, total, cols), bf16, pl.BlockSpec((2, total, block), lambda i: (0, 0, i)))]
    if split:
        outs += [fixed((2, rows, wide), f32), fixed((2, rows, wide), bf16)]
    elif final:
        outs += [fixed((n_x, CORES, rows, feat), bf16)]
    else:
        outs += [fixed(acc_shape, f32)]
    return call(
        body, (count,), ins, outs, deps, scratch=[pltpu.VMEM(acc_shape, f32)], mib=58,
        flops=8 * total * feat * cols, nbytes=8 * feat * cols)


def weight_grad_tile(toks_t, width, block, deps, segments, outs=None):
    feat, n_tok = toks_t[0].shape
    for (start, count), sides in segments:
        parts = [p for side in sides for p in side]
        n, n_side = len(parts), len(sides[0])

        def body(*refs):
            out_refs = refs[-2:]
            for m in range(2):
                total = 0.0
                for c in range(CORES):
                    part = refs[CORES + c * n_side:CORES + (c + 1) * n_side]
                    total = total + dot(refs[c][...], jnp.concatenate([r[m] for r in part], axis=0))
                out_refs[m][...] = total.astype(bf16)

        ins = [(t, pl.BlockSpec(t.shape, lambda i: (0, 0))) for t in toks_t]
        for g, off in parts:
            ins.append((g, pl.BlockSpec((2, g.shape[1], block), lambda i, off=off: (0, 0, off + i))))
        aliases = {}
        if outs is not None:
            aliases = {len(ins): 0, len(ins) + 1: 1}
            ins += [(o, ANY) for o in outs]
        spec = pl.BlockSpec((feat, block), lambda i, start=start: (0, start + i))
        cols = count * block
        outs = call(
            body, (count,), ins, [((feat, width), bf16, spec)] * 2, deps, aliases=aliases,
            flops=8 * feat * n_tok * cols, nbytes=4 * (feat + 2 * n_tok) * cols)
        deps = ()
    return outs


def order_tokens(groups, n_x, deps):
    pieces = [p for group in groups for p in group]
    feat = pieces[0][0].shape[1]
    n_rows = sum(p[0].shape[0] for p in pieces)
    n = len(pieces)

    def body(*refs):
        near_ref, far_ref = refs[2 * n:]
        at, base = 0, 0
        for group in groups:
            for x in range(n_x):
                for k, (a, _) in enumerate(group):
                    rows = a.shape[0] // n_x
                    near, far = refs[base + k], refs[n + base + k]
                    near_ref[:, at:at + rows] = near[x * rows:(x + 1) * rows].astype(f32).T.astype(bf16)
                    far_ref[at:at + rows] = far[x * rows:(x + 1) * rows]
                    at += rows
            base += len(group)

    return call(
        body, (), [(p[k], VMEM) for k in range(2) for p in pieces],
        [((feat, n_rows), bf16, VMEM), ((n_rows, feat), bf16, VMEM)], deps, mib=32)


def transposed(x):
    def body(x_ref, o_ref):
        o_ref[...] = x_ref[...].astype(f32).T.astype(bf16)

    return call(body, (), [(x, VMEM)], [(x.shape[::-1], bf16, VMEM)], mib=32)[0]


def arrange_column(pairs, z, n_x, first, rows):
    feat = pairs[0].shape[2]
    n_tensor = 2 * len(pairs)
    half = n_tensor // n_x // CORES
    shape = (n_x * rows, half * feat)

    def body(z_ref, *refs):
        outs = refs[len(pairs):]
        for s in range(n_tensor):
            for b in range(n_tensor):
                x, f = divmod(b, half * CORES)
                core, k = divmod(f, half)

                @pl.when(z_ref[0] == b ^ s)
                def _():
                    outs[core][x * rows:(x + 1) * rows, k * feat:(k + 1) * feat] = refs[s // 2][s % 2, first:first + rows]

    return call(body, (), [(z, SMEM)] + [(p, VMEM) for p in pairs], [(shape, bf16, VMEM)] * CORES, mib=16)


def after(x, deps):
    def body(x_ref, o_ref):
        o_ref[...] = x_ref[...]

    return call(body, (), [(x, VMEM)], [(x.shape, x.dtype, VMEM)], deps, mib=16)[0]


def make_local(n_tensor, n_dp):
    n_x = n_dp // CORES
    run = n_tensor // n_x
    half = run // CORES
    route = token_route(n_tensor, n_dp)
    route_back = [(b, a) for a, b in route]
    core_swap = [(d, d ^ 1) for d in range(n_dp)]

    def x_shift(s):
        return [(d, (d + CORES * s) % n_dp) for d in range(n_dp)]

    def z_flip(a, k):
        return lax.ppermute(a, "tensor", [(t, t ^ k) for t in range(n_tensor)])

    def swap(a):
        return lax.ppermute(a, "dp", core_swap)

    def send_home(summed):
        return lax.ppermute(summed, ("tensor", "dp"), route_back)

    def gather_column(block, z, pieces):
        if n_tensor != SHORT:
            got = lax.all_gather(block, "tensor", axis=0, tiled=False)
            result = []
            for first, rows in pieces:
                part = got[:, first:first + rows].reshape(n_x, CORES, half, rows, -1).transpose(1, 0, 3, 2, 4)
                part = part.reshape(CORES, n_x * rows, -1)
                result.append((part[0], part[1]))
            return result
        pair = jnp.stack([block, z_flip(block, 1)])
        pairs = [pair, z_flip(pair, 2)]
        return [arrange_column(pairs, z, n_x, first, rows) for first, rows in pieces]

    def reduce_column(blocks):
        blocks = jnp.concatenate(blocks, axis=2)
        rows, feat = blocks.shape[2], blocks.shape[3] // half
        blocks = blocks.reshape(n_x, CORES, rows, half, feat).transpose(0, 1, 3, 2, 4)
        return lax.psum_scatter(
            blocks.reshape(n_tensor, rows, feat), "tensor", scatter_dimension=0, tiled=False)

    def local(tokens, gate_weight, up_weight, grad_hidden, chosen_mask, rejected_mask, margins):
        tok_rows = tokens.shape[0]
        width = gate_weight.shape[1]
        block = BLOCK if width % BLOCK == 0 else width
        n_blocks = width // block
        sizes = [tok_rows * k // 16 for k in SIXTEENTHS]
        begins = [sum(sizes[:q]) for q in range(4)]
        last_split = LAST_SPLIT if sum(LAST_SPLIT) == n_blocks else (n_blocks,)
        pair_weight = -dpo_beta * jax.nn.sigmoid(-dpo_beta * margins)
        token_weight = jnp.broadcast_to(pair_weight[:, None], (margins.shape[0], PAIR_LEN)).reshape(tok_rows)
        token_weight = (token_weight * (chosen_mask - rejected_mask).astype(f32))[:, None]
        z = lax.axis_index("tensor").reshape(1)

        def forward(near_far, mats, deps):
            own, send = forward_tile(*near_far, mats, deps, n_x, block)
            return own, [lax.ppermute(send[s - 1], "dp", x_shift(s)) for s in range(1, n_x)]

        def gates(q, terms, deps, start=0, count=n_blocks):
            return gate_tile(*terms, grad_hidden, token_weight[begins[q]:begins[q] + sizes[q]], deps, block,
                             begins[q], start, count)

        def both_terms(own, got):
            return [[(a, m) for a in [own] + got] for m in range(2)]

        def exchange(mine):
            return [mine] + [lax.ppermute(mine, "dp", x_shift(-s)) for s in range(1, n_x)]

        def rows_of(q, n=1):
            return tokens[begins[q]:begins[q + n - 1] + sizes[q + n - 1]]

        def routed(a):
            return lax.ppermute(a, ("tensor", "dp"), route)

        column = n_tensor == SHORT
        mats = [(gate_weight, swap(gate_weight)), (up_weight, swap(up_weight))]
        weights = [pair[c] for c in range(CORES) for pair in mats]
        t0, t1 = gather_column(routed(rows_of(0, 2)), z, [(0, sizes[0]), (sizes[0], sizes[1])])
        r23 = routed(after(rows_of(2, 2), [t0[0]]))
        own0, got0 = forward(t0, mats, [])
        t2, = gather_column(after(r23[:sizes[2]], [own0]), z, [(0, sizes[2])])
        hidden0, mine0 = gates(0, both_terms(own0, got0), [])
        grads0 = exchange(mine0)
        own1, got1 = forward(t1, mats, [mine0])
        own2, got2 = forward(t2, mats, [own1] + grads0[1:])
        t3, = gather_column(after(r23[sizes[2]:], [t2[0]]), z, [(0, sizes[3])])
        hidden1, mine1 = gates(1, both_terms(own1, got1), [own2])
        grads1 = exchange(mine1)

        def token_grads(grads, deps, before=None, start=0, count=n_blocks, final=True, split=False):
            return token_grad_tile(
                [[g] for g in grads], weights, before, deps, z, n_x, n_tensor, block, start, count, final, split)

        both0, *sums0 = token_grads(grads0, [mine1])
        swapped0 = swap(both0)
        near_t, far_order = order_tokens([[t0], [t1], [t2], [t3]], n_x, [both0])
        far_t = transposed(swap(far_order))
        own3, got3 = forward(t3, mats, [near_t] + got2)
        hidden2, mine2 = gates(2, both_terms(own2, got2), [own3] + grads1[1:])
        grads2 = exchange(mine2)
        hidden3, grads3 = [], []
        deps = [mine2]
        start = 0
        for count in last_split:
            h, mine = gates(3, both_terms(own3, got3), deps, start, count)
            hidden3.append(h)
            grads3.append((exchange(mine), start, count))
            deps = [mine]
            start += count
        deps += [far_t, swapped0]
        both1, *sums1 = token_grads(grads1, deps)
        swapped1 = swap(both1)
        deps = [both1]
        both2, *sums2 = token_grads(grads2, deps)
        swapped2 = swap(both2)
        done = [reduce_column([sums0[0], sums1[0]])]
        deps = [both2]
        before = None
        both3s = []
        for k, (grads, start, count) in enumerate(grads3):
            both3, *sums3 = token_grads(grads, deps, before, start, count, k == len(grads3) - 1)
            before = sums3[0]
            deps = [both3]
            both3s.append((both3, swap(both3), start, count))
        segments = []
        for start, count in FINAL if column and sum(c for _, c in FINAL) == n_blocks else [(0, n_blocks)]:
            for both3, swapped3, at, n in both3s:
                first, stop = max(start, at), min(start + count, at + n)
                if first < stop:
                    segments.append(((first, stop - first), [
                        [(both0, first), (both1, first), (both2, first), (both3, first - at)],
                        [(swapped0, first), (swapped1, first), (swapped2, first), (swapped3, first - at)]]))
        outs = weight_grad_tile([near_t, far_t], width, block, deps + done, segments[:1])
        done.append(reduce_column([sums2[0], sums3[0]]))
        done[0] = after(done[0], [outs[0]])
        outs = weight_grad_tile([near_t, far_t], width, block, [], segments[1:], outs)
        out = send_home(jnp.concatenate(done, axis=0))
        hidden = jnp.concatenate([hidden0, hidden1, hidden2, jnp.concatenate(hidden3, axis=1)], axis=0)
        return (hidden, out, outs[0], outs[1])

    return local


def solution(mesh):
    in_specs = (
        P(("group", "dp"), "tensor"),
        P("dp", "tensor"),
        P("dp", "tensor"),
        P(("group", "dp"), "tensor"),
        P(("group", "dp")),
        P(("group", "dp")),
        P(("group", "dp")),
    )
    out_specs = (P(("group", "dp"), "tensor"),) * 4
    local = make_local(mesh.shape["tensor"], mesh.shape["dp"])
    return jax.shard_map(local, mesh=mesh, in_specs=in_specs, out_specs=out_specs, check_vma=False)
```

profile of v0, /device:TPU:2, one launch (start us, length us, event | category | flops | bytes accessed | tf_op | source)
XLA Modules:
  0.0 357.9 jit_solution(16656314162223643866)
XLA Ops:
  7.8 1.0 slice.45
  8.7 4.5 %collective-permute-start = (bf16[112,1024]{1,0:T(8,128)(2,1)S(1)}, bf16[112,1024]{1,0:T(8,128)(2,1)S(1)}, u32[]{:S(2)}, u32[]{:S(2)}) collective-permute-start(bf16[112,1024]{1,0:T(8,128)(2,1)S(1)} %slice.45), channel_id=1, source_target_pairs={{0,0},{1,5},{2,8},{3,13},{4,4},{5,1},{6,12},{7,9},{8,10},{9,15},{1... | collective-permute-start | bytes 688136 | tf_op jit(solution)/shard_map/ppermute | solution.py:363
  13.2 10.9 %collective-permute-done = bf16[112,1024]{1,0:T(8,128)(2,1)S(1)} collective-permute-done((bf16[112,1024]{1,0:T(8,128)(2,1)S(1)}, bf16[112,1024]{1,0:T(8,128)(2,1)S(1)}, u32[]{:S(2)}, u32[]{:S(2)}) %collective-permute-start) | collective-permute-done | bytes 229408 | tf_op jit(solution)/shard_map/ppermute | solution.py:363
  24.2 6.0 %collective-permute-done.1 = bf16[112,1024]{1,0:T(8,128)(2,1)S(1)} collective-permute-done((bf16[112,1024]{1,0:T(8,128)(2,1)S(1)}, bf16[112,1024]{1,0:T(8,128)(2,1)S(1)}, u32[]{:S(2)}, u32[]{:S(2)}) %collective-permute-start.1) | collective-permute-done | bytes 229408 | tf_op jit(solution)/shard_map/ppermute | solution.py:304
  30.7 1.0 slice.51.refs_0_
  31.7 19.1 %collective-permute-done.2.refs_2_ = bf16[2,112,1024]{2,1,0:T(8,128)(2,1)S(1)} collective-permute-done((bf16[2,112,1024]{2,1,0:T(8,128)(2,1)S(1)}, bf16[2,112,1024]{2,1,0:T(8,128)(2,1)S(1)}, u32[]{:S(2)}, u32[]{:S(2)}) %collective-permute-start.2) | collective-permute-done | bytes 458784 | tf_op jit(solution)/shard_map/ppermute | solution.py:304
  51.0 1.9 collective-permute-start.7
  52.9 14.8 %collective-permute-done.7 = bf16[144,1024]{1,0:T(8,128)(2,1)S(1)} collective-permute-done((bf16[144,1024]{1,0:T(8,128)(2,1)S(1)}, bf16[144,1024]{1,0:T(8,128)(2,1)S(1)}, u32[]{:S(2)}, u32[]{:S(2)}) %collective-permute-start.7) | collective-permute-done | bytes 294944 | tf_op jit(solution)/shard_map/ppermute | solution.py:363
  68.4 12.6 %shard_map.103 = (f32[2,32,3840]{2,1,0:T(8,128)S(1)}, bf16[1,2,32,3840]{3,2,1,0:T(8,128)(2,1)S(1)}) custom-call(bf16[64,1024]{1,0:T(8,128)(2,1)S(1)} %get-tuple-element.42.refs_0_.refs_1_, bf16[64,1024]{1,0:T(8,128)(2,1)S(1)} %get-tuple-element.43.refs_1_.refs_4_, bf16[1024,3840]{1,0:T(8,128)(2,1)} %refs_3_.7, ...), custom_call_target="tpu_custom_call" | custom-call | flops 2013265920 | bytes 31457280 | tf_op jit(solution)/shard_map/pallas_call | solution.py:51
  82.0 4.9 %collective-permute-done.8 = bf16[64,1024]{1,0:T(8,128)(2,1)} collective-permute-done((bf16[64,1024]{1,0:T(8,128)(2,1)S(1)}, bf16[64,1024]{1,0:T(8,128)(2,1)}, u32[]{:S(2)}, u32[]{:S(2)}) %collective-permute-start.8) | collective-permute-done | bytes 131104 | tf_op jit(solution)/shard_map/ppermute | solution.py:304
  86.9 1.6 pad_maximum_fusion.6.refs_1_
  88.7 1.0 copy-done.27
  89.8 1.1 slice.61.refs_0_
  91.0 8.3 %collective-permute-done.9.refs_2_ = bf16[2,64,1024]{2,1,0:T(8,128)(2,1)} collective-permute-done((bf16[2,64,1024]{2,1,0:T(8,128)(2,1)}, bf16[2,64,1024]{2,1,0:T(8,128)(2,1)}, u32[]{:S(2)}, u32[]{:S(2)}) %collective-permute-start.9) | collective-permute-done | bytes 262176 | tf_op jit(solution)/shard_map/ppermute | solution.py:304
  99.3 1.1 shard_map.109
  100.5 2.9 shard_map.104
  104.5 13.6 %shard_map.106 = (f32[2,80,3840]{2,1,0:T(8,128)S(1)}, bf16[1,2,80,3840]{3,2,1,0:T(8,128)(2,1)}) custom-call(bf16[160,1024]{1,0:T(8,128)(2,1)S(1)} %get-tuple-element.47.refs_0_.refs_1_, bf16[160,1024]{1,0:T(8,128)(2,1)S(1)} %get-tuple-element.48.refs_1_.refs_5_, bf16[1024,3840]{1,0:T(8,128)(2,1)} %refs_3_.7, ...), custom_call_target="tpu_custom_call" | custom-call | flops 5033164800 | bytes 31457280 | tf_op jit(solution)/shard_map/pallas_call | solution.py:51
  118.1 1.4 copy-done.3
  119.5 1.7 collective-permute-start.6
  122.0 1.9 collective-permute-start.13
  124.0 13.2 %shard_map.110 = (f32[2,64,3840]{2,1,0:T(8,128)S(1)}, bf16[1,2,64,3840]{3,2,1,0:T(8,128)(2,1)}) custom-call(bf16[128,1024]{1,0:T(8,128)(2,1)S(1)} %get-tuple-element.52.refs_0_.refs_1_.refs_2_, bf16[128,1024]{1,0:T(8,128)(2,1)S(1)} %get-tuple-element.53.refs_1_.refs_6_, bf16[1024,3840]{1,0:T(8,128)(2,1)} %refs_3_.7, ...), custom_call_target="tpu_custom_call" | custom-call | flops 4026531840 | bytes 31457280 | tf_op jit(solution)/shard_map/pallas_call | solution.py:51
  137.2 1.3 copy-done.5
  138.5 1.5 collective-permute-start.11
  140.0 1.2 fusion
  141.3 1.4 shard_map.113
  142.7 7.1 %collective-permute-done.6.refs_1_.refs_3_ = bf16[2,80,3840]{2,1,0:T(8,128)(2,1)} collective-permute-done((bf16[2,80,3840]{2,1,0:T(8,128)(2,1)}, bf16[2,80,3840]{2,1,0:T(8,128)(2,1)}, u32[]{:S(2)}, u32[]{:S(2)}) %collective-permute-start.6) | collective-permute-done | bytes 1228832 | tf_op jit(solution)/shard_map/ppermute | solution.py:347
  149.8 1.5 copy-done.6
  151.4 1.1 copy-done.19
  152.4 4.6 %shard_map.111 = (bf16[80,3840]{1,0:T(8,128)(2,1)S(1)}, bf16[2,80,3840]{2,1,0:T(8,128)(2,1)}) custom-call(f32[2,80,3840]{2,1,0:T(8,128)S(1)} %copy-done.4, bf16[2,80,3840]{2,1,0:T(8,128)(2,1)} %collective-permute-done.6.refs_1_.refs_3_, f32[2,80,3840]{2,1,0:T(8,128)S(1)} %copy-done.4, bf16[2,80,3840]{2,1,0:T(8,128)(2,1)} %collective-permute-done.6.refs_1_.refs_3_, ...), custom_call_target="tpu_custom_call" | custom-call | flops 12288000 | bytes 6144000 | tf_op jit(solution)/shard_map/pallas_call | solution.py:51
  157.9 1.8 collective-permute-start.14
  159.7 16.1 %shard_map.114 = (bf16[2,64,3840]{2,1,0:T(8,128)(2,1)}, bf16[2,2,32,1024]{3,2,1,0:T(8,128)(2,1)}) custom-call(s32[1]{0:T(128)} %bitcast.refs_0_, bf16[2,32,3840]{2,1,0:T(8,128)(2,1)} %copy-done.23, bf16[2,32,3840]{2,1,0:T(8,128)(2,1)} %copy-done.24, bf16[1024,3840]{1,0:T(8,128)(2,1)} %refs_3_.7, bf16[1024,3840]{1,0:T(8,128)(2,1)} %refs_4_.17, ...), custom_call_target="tpu_custom_call" | custom-call | flops 2013265920 | bytes 31457280 | tf_op jit(solution)/shard_map/pallas_call | solution.py:51
  175.8 2.5 shard_map.115
  178.4 14.7 %shard_map.116 = (f32[2,80,3840]{2,1,0:T(8,128)}, bf16[1,2,80,3840]{3,2,1,0:T(8,128)(2,1)}) custom-call(bf16[160,1024]{1,0:T(8,128)(2,1)S(1)} %get-tuple-element.57.refs_3_.refs_0_, bf16[160,1024]{1,0:T(8,128)(2,1)S(1)} %get-tuple-element.58.refs_7_.refs_1_, bf16[1024,3840]{1,0:T(8,128)(2,1)} %refs_3_.7, ...), custom_call_target="tpu_custom_call" | custom-call | flops 5033164800 | bytes 31457280 | tf_op jit(solution)/shard_map/pallas_call | solution.py:51
  193.9 1.8 slice.53.refs_4_
  195.9 1.2 collective-permute-done.14.refs_7_.refs_2_
  197.1 1.1 copy-done.14
  198.2 1.7 copy-done.1
  199.9 1.5 copy-done.7
  201.5 1.3 copy-done.15
  202.8 1.0 copy-done.25
  203.8 2.9 shard_map.117
  207.5 1.7 collective-permute-start.18
  209.3 14.3 %collective-permute-done.15.refs_1_.refs_3_ = bf16[2,80,3840]{2,1,0:T(8,128)(2,1)} collective-permute-done((bf16[2,80,3840]{2,1,0:T(8,128)(2,1)}, bf16[2,80,3840]{2,1,0:T(8,128)(2,1)}, u32[]{:S(2)}, u32[]{:S(2)}) %collective-permute-start.15) | collective-permute-done | bytes 1228832 | tf_op jit(solution)/shard_map/ppermute | solution.py:347
  223.5 1.1 copy-done.20
  224.6 4.6 %shard_map.118 = (bf16[80,3840]{1,0:T(8,128)(2,1)S(1)}, bf16[2,80,3840]{2,1,0:T(8,128)(2,1)}) custom-call(f32[2,80,3840]{2,1,0:T(8,128)S(1)} %copy-done.2, bf16[2,80,3840]{2,1,0:T(8,128)(2,1)} %collective-permute-done.15.refs_1_.refs_3_, f32[2,80,3840]{2,1,0:T(8,128)S(1)} %copy-done.2, bf16[2,80,3840]{2,1,0:T(8,128)(2,1)} %collective-permute-done.15.refs_1_.refs_3_, ...), custom_call_target="tpu_custom_call" | custom-call | flops 12288000 | bytes 6144000 | tf_op jit(solution)/shard_map/pallas_call | solution.py:51
  229.3 1.7 collective-permute-start.19
  231.0 1.6 shard_map.119.refs_8_.refs_1_
  232.6 1.0 copy-done.8
  233.6 17.5 %shard_map.120 = (bf16[2,160,3840]{2,1,0:T(8,128)(2,1)}, bf16[2,2,80,1024]{3,2,1,0:T(8,128)(2,1)}) custom-call(s32[1]{0:T(128)} %bitcast.refs_0_, bf16[2,80,3840]{2,1,0:T(8,128)(2,1)} %get-tuple-element.59.refs_7_.refs_1_, bf16[2,80,3840]{2,1,0:T(8,128)(2,1)} %copy-done.14, bf16[1024,3840]{1,0:T(8,128)(2,1)} %refs_3_.7, bf16[1024,3840]{1,0:T(8,128)(2,1)} %refs_4_.17, ...), custom_call_target="tpu_custom_call" | custom-call | flops 5033164800 | bytes 31457280 | tf_op jit(solution)/shard_map/pallas_call | solution.py:51
  251.0 2.1 pad_maximum_fusion.2
  253.5 17.1 %shard_map.121 = (bf16[2,128,3840]{2,1,0:T(8,128)(2,1)}, bf16[2,2,64,1024]{3,2,1,0:T(8,128)(2,1)}) custom-call(s32[1]{0:T(128)} %bitcast.refs_0_, bf16[2,64,3840]{2,1,0:T(8,128)(2,1)} %get-tuple-element.65.refs_6_.refs_1_, bf16[2,64,3840]{2,1,0:T(8,128)(2,1)} %collective-permute-done.18.refs_2_, bf16[1024,3840]{1,0:T(8,128)(2,1)} %refs_3_.7, ...), custom_call_target="tpu_custom_call" | custom-call | flops 4026531840 | bytes 31457280 | tf_op jit(solution)/shard_map/pallas_call | solution.py:51
  270.6 1.0 copy-done.48
  271.6 17.7 %shard_map.122 = (bf16[2,160,3840]{2,1,0:T(8,128)(2,1)}, bf16[2,2,80,1024]{3,2,1,0:T(8,128)(2,1)}) custom-call(s32[1]{0:T(128)} %bitcast.refs_0_, bf16[2,80,3840]{2,1,0:T(8,128)(2,1)} %get-tuple-element.68.refs_7_.refs_1_, bf16[2,80,3840]{2,1,0:T(8,128)(2,1)} %copy-done.48, bf16[1024,3840]{1,0:T(8,128)(2,1)} %refs_3_.7, bf16[1024,3840]{1,0:T(8,128)(2,1)} %refs_4_.17, ...), custom_call_target="tpu_custom_call" | custom-call | flops 5033164800 | bytes 31457280 | tf_op jit(solution)/shard_map/pallas_call | solution.py:51
  289.9 2.2 pad_maximum_fusion.1
  292.2 4.9 %collective-permute-done.21.refs_8_ = bf16[2,128,3840]{2,1,0:T(8,128)(2,1)} collective-permute-done((bf16[2,128,3840]{2,1,0:T(8,128)(2,1)S(1)}, bf16[2,128,3840]{2,1,0:T(8,128)(2,1)}, u32[]{:S(2)}, u32[]{:S(2)}) %collective-permute-start.21) | collective-permute-done | bytes 1966112 | tf_op jit(solution)/shard_map/ppermute | solution.py:307
  297.1 1.2 copy-done.17
  299.3 16.8 %shard_map.123 = (bf16[1024,3840]{1,0:T(8,128)(2,1)}, bf16[1024,3840]{1,0:T(8,128)(2,1)}) custom-call(bf16[1024,512]{1,0:T(8,128)(2,1)S(1)} %copy-done.17, bf16[1024,512]{1,0:T(8,128)(2,1)S(1)} %copy-done.9, bf16[2,64,3840]{2,1,0:T(8,128)(2,1)} %get-tuple-element.60.refs_8_.refs_2_, bf16[2,160,3840]{2,1,0:T(8,128)(2,1)} %get-tuple-element.71.refs_7_.refs_3_, ...), custom_call_target="tpu_custom_call" | custom-call | flops 12884901888 | bytes 25165824 | tf_op jit(solution)/shard_map/pallas_call | solution.py:51
  316.1 3.3 copy-done
  319.4 1.8 reduce-scatter.5.cloned.1.call-done
  321.2 1.0 pad_maximum_fusion.3
  322.2 3.0 collective-permute-start.23
  325.3 1.4 pad_maximum_fusion
  327.8 6.7 %shard_map.125 = (bf16[1024,3840]{1,0:T(8,128)(2,1)}, bf16[1024,3840]{1,0:T(8,128)(2,1)}) custom-call(bf16[1024,512]{1,0:T(8,128)(2,1)S(1)} %copy-done.18, bf16[1024,512]{1,0:T(8,128)(2,1)S(1)} %copy-done.9, bf16[2,64,3840]{2,1,0:T(8,128)(2,1)} %get-tuple-element.60.refs_8_.refs_2_, ...), custom_call_target="tpu_custom_call", output_to_operand_aliasing={{0}: (10, {}), {1}: (11, {})} | custom-call | flops 3221225472 | bytes 6291456 | tf_op jit(solution)/shard_map/pallas_call | solution.py:51
  334.6 15.8 %collective-permute-done.23 = bf16[256,1024]{1,0:T(8,128)(2,1)S(1)} collective-permute-done((bf16[256,1024]{1,0:T(8,128)(2,1)S(1)}, bf16[256,1024]{1,0:T(8,128)(2,1)S(1)}, u32[]{:S(2)}, u32[]{:S(2)}) %collective-permute-start.23) | collective-permute-done | bytes 524320 | tf_op jit(solution)/shard_map/ppermute | solution.py:310
  (149 shorter events, 11.9 us)
Async XLA Ops:
  7.2 285.0 %reduce-scatter.3.cloned.1.call-start = ((), (), s32[]{:S(2)}) async-start(), calls=%async_computation.2 | async-start | bytes 1146880 | tf_op jit(solution)/shard_map/reduce_scatter | solution.py:329
  7.2 60.5 %collective-permute-start.3 = (bf16[1024,3840]{1,0:T(8,128)(2,1)}, bf16[1024,3840]{1,0:T(8,128)(2,1)}, u32[]{:S(2)}, u32[]{:S(2)}) collective-permute-start(bf16[1024,3840]{1,0:T(8,128)(2,1)} %refs_3_.7), channel_id=1, source_target_pairs={{0,1},{1,0},{2,3},{3,2},{4,5},{5,4},{6,7},{7,6},{8,9},{9,8},{10,11... | collective-permute-start | bytes 23592968 | tf_op jit(solution)/shard_map/ppermute | solution.py:307
  7.3 60.4 %collective-permute-start.4 = (bf16[1024,3840]{1,0:T(8,128)(2,1)}, bf16[1024,3840]{1,0:T(8,128)(2,1)}, u32[]{:S(2)}, u32[]{:S(2)}) collective-permute-start(bf16[1024,3840]{1,0:T(8,128)(2,1)} %refs_4_.17), channel_id=1, source_target_pairs={{0,1},{1,0},{2,3},{3,2},{4,5},{5,4},{6,7},{7,6},{8,9},{9,8},{10,11... | collective-permute-start | bytes 23592968 | tf_op jit(solution)/shard_map/ppermute | solution.py:307
  8.7 15.4 %collective-permute-start = (bf16[112,1024]{1,0:T(8,128)(2,1)S(1)}, bf16[112,1024]{1,0:T(8,128)(2,1)S(1)}, u32[]{:S(2)}, u32[]{:S(2)}) collective-permute-start(bf16[112,1024]{1,0:T(8,128)(2,1)S(1)} %slice.45), channel_id=1, source_target_pairs={{0,0},{1,5},{2,8},{3,13},{4,4},{5,1},{6,12},{7,9},{8,10},{9,15},{1... | collective-permute-start | bytes 688136 | tf_op jit(solution)/shard_map/ppermute | solution.py:363
  24.2 6.0 %collective-permute-start.1 = (bf16[112,1024]{1,0:T(8,128)(2,1)S(1)}, bf16[112,1024]{1,0:T(8,128)(2,1)S(1)}, u32[]{:S(2)}, u32[]{:S(2)}) collective-permute-start(bf16[112,1024]{1,0:T(8,128)(2,1)S(1)} %collective-permute-done), channel_id=1, source_target_pairs={{0,4},{4,0},{8,12},{12,8},{1,5},{5,1},{9,13},{13,9},{2,6},{6,2},{1... | collective-permute-start | bytes 688136 | tf_op jit(solution)/shard_map/ppermute | solution.py:304
  30.2 20.6 %collective-permute-start.2 = (bf16[2,112,1024]{2,1,0:T(8,128)(2,1)S(1)}, bf16[2,112,1024]{2,1,0:T(8,128)(2,1)S(1)}, u32[]{:S(2)}, u32[]{:S(2)}) collective-permute-start(bf16[2,112,1024]{2,1,0:T(8,128)(2,1)S(1)} %pad_maximum_fusion.4.refs_1_), channel_id=1, source_target_pairs={{0,8},{4,12},{8,0},{12,4},{1,9},{5,13},{9,1},{13,5},{2,10},{6,14},... | collective-permute-start | bytes 1376264 | tf_op jit(solution)/shard_map/ppermute | solution.py:304
  50.8 16.9 %copy-start.26 = (bf16[2,112,1024]{2,1,0:T(8,128)(2,1)}, bf16[2,112,1024]{2,1,0:T(8,128)(2,1)S(1)}, u32[]{:S(2)}) copy-start(bf16[2,112,1024]{2,1,0:T(8,128)(2,1)S(1)} %collective-permute-done.2.refs_2_) | copy-start | bytes 1376260
  50.9 30.1 %copy-start.32 = (bf16[64,1024]{1,0:T(8,128)(2,1)}, bf16[64,1024]{1,0:T(8,128)(2,1)S(1)}, u32[]{:S(2)}) copy-start(bf16[64,1024]{1,0:T(8,128)(2,1)S(1)} %get-tuple-element.42.refs_0_.refs_1_) | copy-start | bytes 393220
  50.9 30.1 %copy-start.40 = (bf16[64,1024]{1,0:T(8,128)(2,1)}, bf16[64,1024]{1,0:T(8,128)(2,1)S(1)}, u32[]{:S(2)}) copy-start(bf16[64,1024]{1,0:T(8,128)(2,1)S(1)} %get-tuple-element.43.refs_1_.refs_4_) | copy-start | bytes 393220
  51.0 16.7 %collective-permute-start.7 = (bf16[144,1024]{1,0:T(8,128)(2,1)S(1)}, bf16[144,1024]{1,0:T(8,128)(2,1)S(1)}, u32[]{:S(2)}, u32[]{:S(2)}) collective-permute-start(bf16[144,1024]{1,0:T(8,128)(2,1)S(1)} %shard_map.107), channel_id=1, source_target_pairs={{0,0},{1,5},{2,8},{3,13},{4,4},{5,1},{6,12},{7,9},{8,10},{9,15},{1... | collective-permute-start | bytes 884744 | tf_op jit(solution)/shard_map/ppermute | solution.py:363
  68.4 13.4 %copy-start.54 = (f32[4]{0:T(128)S(1)}, f32[4]{0:T(128)}, u32[]{:S(2)}) copy-start(f32[4]{0:T(128)} %param.13) | copy-start | bytes 52
  68.4 20.1 %copy-start.52 = (s32[256]{0:T(256)S(1)}, s32[256]{0:T(256)}, u32[]{:S(2)}) copy-start(s32[256]{0:T(256)} %param.11) | copy-start | bytes 3076
  68.4 20.1 %copy-start.53 = (s32[256]{0:T(256)S(1)}, s32[256]{0:T(256)}, u32[]{:S(2)}) copy-start(s32[256]{0:T(256)} %param.12) | copy-start | bytes 3076
  81.1 19.5 %copy-start.12 = (bf16[256,3840]{1,0:T(8,128)(2,1)S(1)}, bf16[256,3840]{1,0:T(8,128)(2,1)}, u32[]{:S(2)}) copy-start(bf16[256,3840]{1,0:T(8,128)(2,1)} %refs_4_.10) | copy-start | bytes 5898244
  81.8 5.1 %collective-permute-start.8 = (bf16[64,1024]{1,0:T(8,128)(2,1)S(1)}, bf16[64,1024]{1,0:T(8,128)(2,1)}, u32[]{:S(2)}, u32[]{:S(2)}) collective-permute-start(bf16[64,1024]{1,0:T(8,128)(2,1)S(1)} %shard_map.108), channel_id=1, source_target_pairs={{0,4},{4,0},{8,12},{12,8},{1,5},{5,1},{9,13},{13,9},{2,6},{6,2},{1... | collective-permute-start | bytes 393224 | tf_op jit(solution)/shard_map/ppermute | solution.py:304
  82.0 18.5 %collective-permute-start.5 = (bf16[2,32,3840]{2,1,0:T(8,128)(2,1)}, bf16[2,32,3840]{2,1,0:T(8,128)(2,1)}, u32[]{:S(2)}, u32[]{:S(2)}) collective-permute-start(bf16[2,32,3840]{2,1,0:T(8,128)(2,1)} %bitcast.27), channel_id=1, source_target_pairs={{0,2},{1,3},{2,0},{3,1},{4,6},{5,7},{6,4},{7,5},{8,10},{9,11},{10,... | collective-permute-start | bytes 1474568 | tf_op jit(solution)/shard_map/ppermute | solution.py:347
  88.5 10.7 %collective-permute-start.9 = (bf16[2,64,1024]{2,1,0:T(8,128)(2,1)}, bf16[2,64,1024]{2,1,0:T(8,128)(2,1)}, u32[]{:S(2)}, u32[]{:S(2)}) collective-permute-start(bf16[2,64,1024]{2,1,0:T(8,128)(2,1)} %pad_maximum_fusion.6.refs_1_), channel_id=1, source_target_pairs={{0,8},{4,12},{8,0},{12,4},{1,9},{5,13},{9,1},{13,5},{2,10},{6,14},... | collective-permute-start | bytes 786440 | tf_op jit(solution)/shard_map/ppermute | solution.py:304
  89.8 14.7 %copy-start.28 = (bf16[160,1024]{1,0:T(8,128)(2,1)}, bf16[160,1024]{1,0:T(8,128)(2,1)S(1)}, u32[]{:S(2)}) copy-start(bf16[160,1024]{1,0:T(8,128)(2,1)S(1)} %get-tuple-element.47.refs_0_.refs_1_) | copy-start | bytes 983044
  89.8 14.7 %copy-start.30 = (bf16[160,1024]{1,0:T(8,128)(2,1)}, bf16[160,1024]{1,0:T(8,128)(2,1)S(1)}, u32[]{:S(2)}) copy-start(bf16[160,1024]{1,0:T(8,128)(2,1)S(1)} %get-tuple-element.48.refs_1_.refs_5_) | copy-start | bytes 983044
  100.4 23.6 %copy-start.21 = (bf16[128,1024]{1,0:T(8,128)(2,1)}, bf16[128,1024]{1,0:T(8,128)(2,1)S(1)}, u32[]{:S(2)}) copy-start(bf16[128,1024]{1,0:T(8,128)(2,1)S(1)} %get-tuple-element.52.refs_0_.refs_1_.refs_2_) | copy-start | bytes 786436
  100.4 23.6 %copy-start.34 = (bf16[128,1024]{1,0:T(8,128)(2,1)}, bf16[128,1024]{1,0:T(8,128)(2,1)S(1)}, u32[]{:S(2)}) copy-start(bf16[128,1024]{1,0:T(8,128)(2,1)S(1)} %get-tuple-element.53.refs_1_.refs_6_) | copy-start | bytes 786436
  100.5 20.8 %collective-permute-start.12 = (bf16[80,1024]{1,0:T(8,128)(2,1)S(1)}, bf16[80,1024]{1,0:T(8,128)(2,1)S(1)}, u32[]{:S(2)}, u32[]{:S(2)}) collective-permute-start(bf16[80,1024]{1,0:T(8,128)(2,1)S(1)} %shard_map.112), channel_id=1, source_target_pairs={{0,4},{4,0},{8,12},{12,8},{1,5},{5,1},{9,13},{13,9},{2,6},{6,2},{1... | collective-permute-start | bytes 491528 | tf_op jit(solution)/shard_map/ppermute | solution.py:304
  104.1 13.9 %copy-start.23 = (bf16[2,32,3840]{2,1,0:T(8,128)(2,1)}, bf16[2,32,3840]{2,1,0:T(8,128)(2,1)S(1)}, u32[]{:S(2)}) copy-start(bf16[2,32,3840]{2,1,0:T(8,128)(2,1)S(1)} %get-tuple-element.49.refs_6_.refs_1_) | copy-start | bytes 1474564
  104.1 19.8 %collective-permute-start.10 = (bf16[2,32,3840]{2,1,0:T(8,128)(2,1)S(1)}, bf16[2,32,3840]{2,1,0:T(8,128)(2,1)S(1)}, u32[]{:S(2)}, u32[]{:S(2)}) collective-permute-start(bf16[2,32,3840]{2,1,0:T(8,128)(2,1)S(1)} %get-tuple-element.49.refs_6_.refs_1_), channel_id=1, source_target_pairs={{0,2},{1,3},{2,0},{3,1},{4,6},{5,7},{6,4},{7,5},{8,10},{9,11},{10,... | collective-permute-start | bytes 1474568 | tf_op jit(solution)/shard_map/ppermute | solution.py:357
  119.5 30.3 %collective-permute-start.6 = (bf16[2,80,3840]{2,1,0:T(8,128)(2,1)}, bf16[2,80,3840]{2,1,0:T(8,128)(2,1)}, u32[]{:S(2)}, u32[]{:S(2)}) collective-permute-start(bf16[2,80,3840]{2,1,0:T(8,128)(2,1)} %bitcast.5), channel_id=1, source_target_pairs={{0,2},{1,3},{2,0},{3,1},{4,6},{5,7},{6,4},{7,5},{8,10},{9,11},{10,... | collective-permute-start | bytes 3686408 | tf_op jit(solution)/shard_map/ppermute | solution.py:347
  122.0 19.3 %collective-permute-start.13 = (bf16[2,80,1024]{2,1,0:T(8,128)(2,1)}, bf16[2,80,1024]{2,1,0:T(8,128)(2,1)}, u32[]{:S(2)}, u32[]{:S(2)}) collective-permute-start(bf16[2,80,1024]{2,1,0:T(8,128)(2,1)} %pad_maximum_fusion.5.refs_1_), channel_id=1, source_target_pairs={{0,8},{4,12},{8,0},{12,4},{1,9},{5,13},{9,1},{13,5},{2,10},{6,14},... | collective-permute-start | bytes 983048 | tf_op jit(solution)/shard_map/ppermute | solution.py:304
  124.0 13.2 %copy-start.24 = (bf16[2,32,3840]{2,1,0:T(8,128)(2,1)}, bf16[2,32,3840]{2,1,0:T(8,128)(2,1)S(1)}, u32[]{:S(2)}) copy-start(bf16[2,32,3840]{2,1,0:T(8,128)(2,1)S(1)} %collective-permute-done.10.refs_7_.refs_2_) | copy-start | bytes 1474564
  124.0 16.0 %copy-start.13 = (bf16[256,3840]{1,0:T(8,128)(2,1)S(1)}, bf16[256,3840]{1,0:T(8,128)(2,1)}, u32[]{:S(2)}) copy-start(bf16[256,3840]{1,0:T(8,128)(2,1)} %refs_4_.10) | copy-start | bytes 5898244
  138.5 11.3 %copy-start.4 = (f32[2,80,3840]{2,1,0:T(8,128)S(1)}, f32[2,80,3840]{2,1,0:T(8,128)}, u32[]{:S(2)}) copy-start(f32[2,80,3840]{2,1,0:T(8,128)} %copy-done.3) | copy-start | bytes 7372804
  138.5 39.9 %collective-permute-start.11 = (bf16[2,64,3840]{2,1,0:T(8,128)(2,1)}, bf16[2,64,3840]{2,1,0:T(8,128)(2,1)S(1)}, u32[]{:S(2)}, u32[]{:S(2)}) collective-permute-start(bf16[2,64,3840]{2,1,0:T(8,128)(2,1)} %bitcast.9), channel_id=1, source_target_pairs={{0,2},{1,3},{2,0},{3,1},{4,6},{5,7},{6,4},{7,5},{8,10},{9,11},{10,... | collective-permute-start | bytes 2949128 | tf_op jit(solution)/shard_map/ppermute | solution.py:347
  149.8 1.5 copy-start.6
  157.9 17.8 %copy-start.22 = (bf16[128,1024]{1,0:T(8,128)(2,1)S(1)}, bf16[128,1024]{1,0:T(8,128)(2,1)}, u32[]{:S(2)}) copy-start(bf16[128,1024]{1,0:T(8,128)(2,1)} %copy-done.21) | copy-start | bytes 786436
  157.9 17.9 %copy-start.29 = (bf16[160,1024]{1,0:T(8,128)(2,1)S(1)}, bf16[160,1024]{1,0:T(8,128)(2,1)}, u32[]{:S(2)}) copy-start(bf16[160,1024]{1,0:T(8,128)(2,1)} %copy-done.28) | copy-start | bytes 983044
  157.9 17.9 %copy-start.31 = (bf16[160,1024]{1,0:T(8,128)(2,1)S(1)}, bf16[160,1024]{1,0:T(8,128)(2,1)}, u32[]{:S(2)}) copy-start(bf16[160,1024]{1,0:T(8,128)(2,1)} %copy-done.30) | copy-start | bytes 983044
  157.9 17.9 %copy-start.33 = (bf16[64,1024]{1,0:T(8,128)(2,1)S(1)}, bf16[64,1024]{1,0:T(8,128)(2,1)}, u32[]{:S(2)}) copy-start(bf16[64,1024]{1,0:T(8,128)(2,1)} %copy-done.32) | copy-start | bytes 393220
  157.9 17.9 %copy-start.35 = (bf16[128,1024]{1,0:T(8,128)(2,1)S(1)}, bf16[128,1024]{1,0:T(8,128)(2,1)}, u32[]{:S(2)}) copy-start(bf16[128,1024]{1,0:T(8,128)(2,1)} %copy-done.34) | copy-start | bytes 786436
  157.9 17.9 %copy-start.41 = (bf16[64,1024]{1,0:T(8,128)(2,1)S(1)}, bf16[64,1024]{1,0:T(8,128)(2,1)}, u32[]{:S(2)}) copy-start(bf16[64,1024]{1,0:T(8,128)(2,1)} %copy-done.40) | copy-start | bytes 393220
  157.9 39.2 %collective-permute-start.14 = (bf16[2,80,3840]{2,1,0:T(8,128)(2,1)}, bf16[2,80,3840]{2,1,0:T(8,128)(2,1)S(1)}, u32[]{:S(2)}, u32[]{:S(2)}) collective-permute-start(bf16[2,80,3840]{2,1,0:T(8,128)(2,1)} %get-tuple-element.59.refs_7_.refs_1_), channel_id=1, source_target_pairs={{0,2},{1,3},{2,0},{3,1},{4,6},{5,7},{6,4},{7,5},{8,10},{9,11},{10,... | collective-permute-start | bytes 3686408 | tf_op jit(solution)/shard_map/ppermute | solution.py:357
  178.3 14.7 %copy-start.16 = (bf16[1024,512]{1,0:T(8,128)(2,1)}, bf16[1024,512]{1,0:T(8,128)(2,1)S(1)}, u32[]{:S(2)}) copy-start(bf16[1024,512]{1,0:T(8,128)(2,1)S(1)} %get-tuple-element.61.refs_6_.refs_0_) | copy-start | bytes 3145732
  193.0 30.5 %collective-permute-start.15 = (bf16[2,80,3840]{2,1,0:T(8,128)(2,1)}, bf16[2,80,3840]{2,1,0:T(8,128)(2,1)}, u32[]{:S(2)}, u32[]{:S(2)}) collective-permute-start(bf16[2,80,3840]{2,1,0:T(8,128)(2,1)} %bitcast.13), channel_id=1, source_target_pairs={{0,2},{1,3},{2,0},{3,1},{4,6},{5,7},{6,4},{7,5},{8,10},{9,11},{10,... | collective-permute-start | bytes 3686408 | tf_op jit(solution)/shard_map/ppermute | solution.py:347
  193.4 37.6 %collective-permute-start.16 = (bf16[512,1024]{1,0:T(8,128)(2,1)}, bf16[512,1024]{1,0:T(8,128)(2,1)}, u32[]{:S(2)}, u32[]{:S(2)}) collective-permute-start(bf16[512,1024]{1,0:T(8,128)(2,1)} %get-tuple-element.69), channel_id=1, source_target_pairs={{0,1},{1,0},{2,3},{3,2},{4,5},{5,4},{6,7},{7,6},{8,9},{9,8},{10,11... | collective-permute-start | bytes 3145736 | tf_op jit(solution)/shard_map/ppermute | solution.py:307
  193.4 40.2 %collective-permute-start.17 = (bf16[2,64,3840]{2,1,0:T(8,128)(2,1)}, bf16[2,64,3840]{2,1,0:T(8,128)(2,1)}, u32[]{:S(2)}, u32[]{:S(2)}) collective-permute-start(bf16[2,64,3840]{2,1,0:T(8,128)(2,1)} %get-tuple-element.60.refs_8_.refs_2_), channel_id=1, source_target_pairs={{0,1},{1,0},{2,3},{3,2},{4,5},{5,4},{6,7},{7,6},{8,9},{9,8},{10,11... | collective-permute-start | bytes 2949128 | tf_op jit(solution)/shard_map/ppermute | solution.py:307
  198.2 1.7 copy-start.1
  199.9 1.5 copy-start.7
  203.8 19.7 %copy-start.2 = (f32[2,80,3840]{2,1,0:T(8,128)S(1)}, f32[2,80,3840]{2,1,0:T(8,128)}, u32[]{:S(2)}) copy-start(f32[2,80,3840]{2,1,0:T(8,128)} %get-tuple-element.62.refs_6_.refs_0_.refs_2_) | copy-start | bytes 7372804
  207.5 46.0 %collective-permute-start.18 = (bf16[2,64,3840]{2,1,0:T(8,128)(2,1)}, bf16[2,64,3840]{2,1,0:T(8,128)(2,1)}, u32[]{:S(2)}, u32[]{:S(2)}) collective-permute-start(bf16[2,64,3840]{2,1,0:T(8,128)(2,1)} %get-tuple-element.65.refs_6_.refs_1_), channel_id=1, source_target_pairs={{0,2},{1,3},{2,0},{3,1},{4,6},{5,7},{6,4},{7,5},{8,10},{9,11},{10,... | collective-permute-start | bytes 2949128 | tf_op jit(solution)/shard_map/ppermute | solution.py:357
  229.3 3.3 copy-start.38
  229.3 41.3 %collective-permute-start.19 = (bf16[2,80,3840]{2,1,0:T(8,128)(2,1)}, bf16[2,80,3840]{2,1,0:T(8,128)(2,1)S(1)}, u32[]{:S(2)}, u32[]{:S(2)}) collective-permute-start(bf16[2,80,3840]{2,1,0:T(8,128)(2,1)} %get-tuple-element.68.refs_7_.refs_1_), channel_id=1, source_target_pairs={{0,2},{1,3},{2,0},{3,1},{4,6},{5,7},{6,4},{7,5},{8,10},{9,11},{10,... | collective-permute-start | bytes 3686408 | tf_op jit(solution)/shard_map/ppermute | solution.py:357
  233.5 17.5 %copy-start.51 = (bf16[2,2,32,1024]{3,2,1,0:T(8,128)(2,1)S(1)}, bf16[2,2,32,1024]{3,2,1,0:T(8,128)(2,1)}, u32[]{:S(2)}) copy-start(bf16[2,2,32,1024]{3,2,1,0:T(8,128)(2,1)} %get-tuple-element.67) | copy-start | bytes 786436
  253.1 68.1 %reduce-scatter.5.cloned.1.call-start = ((), (), s32[]{:S(2)}) async-start(), calls=%async_computation.3 | async-start | bytes 1474560 | tf_op jit(solution)/shard_map/reduce_scatter | solution.py:329
  253.4 38.7 %collective-permute-start.20 = (bf16[2,160,3840]{2,1,0:T(8,128)(2,1)}, bf16[2,160,3840]{2,1,0:T(8,128)(2,1)}, u32[]{:S(2)}, u32[]{:S(2)}) collective-permute-start(bf16[2,160,3840]{2,1,0:T(8,128)(2,1)} %get-tuple-element.71.refs_7_.refs_3_), channel_id=1, source_target_pairs={{0,1},{1,0},{2,3},{3,2},{4,5},{5,4},{6,7},{7,6},{8,9},{9,8},{10,11... | collective-permute-start | bytes 7372808 | tf_op jit(solution)/shard_map/ppermute | solution.py:307
  271.6 18.2 %copy-start.10 = (bf16[2,128,3840]{2,1,0:T(8,128)(2,1)S(1)}, bf16[2,128,3840]{2,1,0:T(8,128)(2,1)}, u32[]{:S(2)}) copy-start(bf16[2,128,3840]{2,1,0:T(8,128)(2,1)} %get-tuple-element.72.refs_7_.refs_4_) | copy-start | bytes 5898244
  271.6 18.3 %copy-start.49 = (bf16[2,2,64,1024]{3,2,1,0:T(8,128)(2,1)S(1)}, bf16[2,2,64,1024]{3,2,1,0:T(8,128)(2,1)}, u32[]{:S(2)}) copy-start(bf16[2,2,64,1024]{3,2,1,0:T(8,128)(2,1)} %get-tuple-element.75) | copy-start | bytes 1572868
  289.3 7.8 %copy-start.9 = (bf16[1024,512]{1,0:T(8,128)(2,1)S(1)}, bf16[1024,512]{1,0:T(8,128)(2,1)}, u32[]{:S(2)}) copy-start(bf16[1024,512]{1,0:T(8,128)(2,1)} %copy-done.8) | copy-start | bytes 3145732
  289.3 7.8 %collective-permute-start.22 = (bf16[2,160,3840]{2,1,0:T(8,128)(2,1)}, bf16[2,160,3840]{2,1,0:T(8,128)(2,1)}, u32[]{:S(2)}, u32[]{:S(2)}) collective-permute-start(bf16[2,160,3840]{2,1,0:T(8,128)(2,1)} %get-tuple-element.73.refs_5_.refs_10_), channel_id=1, source_target_pairs={{0,1},{1,0},{2,3},{3,2},{4,5},{5,4},{6,7},{7,6},{8,9},{9,8},{10,11... | collective-permute-start | bytes 7372808 | tf_op jit(solution)/shard_map/ppermute | solution.py:307
  289.8 7.2 %collective-permute-start.21 = (bf16[2,128,3840]{2,1,0:T(8,128)(2,1)S(1)}, bf16[2,128,3840]{2,1,0:T(8,128)(2,1)}, u32[]{:S(2)}, u32[]{:S(2)}) collective-permute-start(bf16[2,128,3840]{2,1,0:T(8,128)(2,1)S(1)} %copy-done.10), channel_id=1, source_target_pairs={{0,1},{1,0},{2,3},{3,2},{4,5},{5,4},{6,7},{7,6},{8,9},{9,8},{10,11... | collective-permute-start | bytes 5898248 | tf_op jit(solution)/shard_map/ppermute | solution.py:307
  316.1 3.3 copy-start
  319.4 5.9 %copy-start.37 = (bf16[80,3840]{1,0:T(8,128)(2,1)S(1)}, bf16[80,3840]{1,0:T(8,128)(2,1)}, u32[]{:S(2)}) copy-start(bf16[80,3840]{1,0:T(8,128)(2,1)} %copy-done.36) | copy-start | bytes 1843204
  319.4 5.9 %copy-start.39 = (bf16[80,3840]{1,0:T(8,128)(2,1)S(1)}, bf16[80,3840]{1,0:T(8,128)(2,1)}, u32[]{:S(2)}) copy-start(bf16[80,3840]{1,0:T(8,128)(2,1)} %copy-done.38) | copy-start | bytes 1843204
  319.4 5.9 %copy-start.43 = (bf16[64,3840]{1,0:T(8,128)(2,1)S(1)}, bf16[64,3840]{1,0:T(8,128)(2,1)}, u32[]{:S(2)}) copy-start(bf16[64,3840]{1,0:T(8,128)(2,1)} %copy-done.42) | copy-start | bytes 1474564
  319.4 5.9 %copy-start.45 = (bf16[32,3840]{1,0:T(8,128)(2,1)S(1)}, bf16[32,3840]{1,0:T(8,128)(2,1)}, u32[]{:S(2)}) copy-start(bf16[32,3840]{1,0:T(8,128)(2,1)} %copy-done.44) | copy-start | bytes 737284
  322.2 28.1 %collective-permute-start.23 = (bf16[256,1024]{1,0:T(8,128)(2,1)S(1)}, bf16[256,1024]{1,0:T(8,128)(2,1)S(1)}, u32[]{:S(2)}, u32[]{:S(2)}) collective-permute-start(bf16[256,1024]{1,0:T(8,128)(2,1)S(1)} %pad_maximum_fusion.3), channel_id=1, source_target_pairs={{0,0},{5,1},{8,2},{13,3},{4,4},{1,5},{12,6},{9,7},{10,8},{15,9},{2... | collective-permute-start | bytes 1572872 | tf_op jit(solution)/shard_map/ppermute | solution.py:310
  325.3 2.3 copy-start.11
  325.3 2.5 copy-start.18
  (17 other events, 17.4 us)
Sparse Core Ops, SparseCore 0:
  253.3 24.7 reduce-scatter.2
  292.2 28.9 reduce-scatter.4
where the time goes:
time: 359 us; the launch traced here: 358 us
  Pallas kernels  168 us (47%)
  waiting for transfers between devices  109 us (30%)
  local copies, waits for them, and re-layouts  34.1 us (9%)
  starting transfers between devices  23 us (6%)
  between operations  14.6 us (4%)
  other arithmetic  9.14 us (3%)
    pallas_call x24, Pallas kernels, call(): pl.pallas_call(wrapped, grid=grid, in_specs=[spec for _, spec in ins] + [...  168 us
    ppermute x6, waiting for transfers between devices, z_flip(): return lax.ppermute(a, 'tensor', [(t, t ^ k) for t in range(n_tensor)])  38.3 us
    unnamed x111, local copies, waits for them, and re-layouts  27.3 us
    ppermute x2, waiting for transfers between devices, routed(): return lax.ppermute(a, ('tensor', 'dp'), route)  25.7 us
    ppermute x4, waiting for transfers between devices, forward(): lax.ppermute(send[s - 1], 'dp', x_shift(s))  21.3 us
    ppermute x1, waiting for transfers between devices, send_home(): return lax.ppermute(summed, ('tensor', 'dp'), route_back)  15.8 us
  transfers between devices with their start and end apart: 26, of which 12 were waited for; matrix products, arithmetic and copies ran while one was open for 4% of the time, Pallas kernels for 43%

commit v1 on v0

--- a/solution.py
+++ b/solution.py
@@ -366,14 +366,15 @@
         mats = [(gate_weight, swap(gate_weight)), (up_weight, swap(up_weight))]
         weights = [pair[c] for c in range(CORES) for pair in mats]
         t0, t1 = gather_column(routed(rows_of(0, 2)), z, [(0, sizes[0]), (sizes[0], sizes[1])])
-        r23 = routed(after(rows_of(2, 2), [t0[0]]))
+        r2 = routed(rows_of(2))
         own0, got0 = forward(t0, mats, [])
-        t2, = gather_column(after(r23[:sizes[2]], [own0]), z, [(0, sizes[2])])
+        r3 = routed(after(rows_of(3), [own0]))
         hidden0, mine0 = gates(0, both_terms(own0, got0), [])
         grads0 = exchange(mine0)
+        t2, = gather_column(after(r2, [mine0]), z, [(0, sizes[2])])
         own1, got1 = forward(t1, mats, [mine0])
         own2, got2 = forward(t2, mats, [own1] + grads0[1:])
-        t3, = gather_column(after(r23[sizes[2]:], [t2[0]]), z, [(0, sizes[3])])
+        t3, = gather_column(after(r3, [t2[0]]), z, [(0, sizes[3])])
         hidden1, mine1 = gates(1, both_terms(own1, got1), [own2])
         grads1 = exchange(mine1)
 
@@ -411,20 +412,22 @@
             both3, *sums3 = token_grads(grads, deps, before, start, count, k == len(grads3) - 1)
             before = sums3[0]
             deps = [both3]
-            both3s.append((both3, swap(both3), start, count))
+            both3s.append((grads, [swap(g) for g in grads], start, count))
         segments = []
         for start, count in FINAL if column and sum(c for _, c in FINAL) == n_blocks else [(0, n_blocks)]:
             for both3, swapped3, at, n in both3s:
                 first, stop = max(start, at), min(start + count, at + n)
                 if first < stop:
                     segments.append(((first, stop - first), [
-                        [(both0, first), (both1, first), (both2, first), (both3, first - at)],
-                        [(swapped0, first), (swapped1, first), (swapped2, first), (swapped3, first - at)]]))
+                        [(both0, first), (both1, first), (both2, first)] + [(g, first - at) for g in both3],
+                        [(swapped0, first), (swapped1, first), (swapped2, first)] + [(g, first - at) for g in swapped3]]))
         outs = weight_grad_tile([near_t, far_t], width, block, deps + done, segments[:1])
         done.append(reduce_column([sums2[0], sums3[0]]))
-        done[0] = after(done[0], [outs[0]])
-        outs = weight_grad_tile([near_t, far_t], width, block, [], segments[1:], outs)
-        out = send_home(jnp.concatenate(done, axis=0))
+        out1 = send_home(done[0][sizes[0]:])
+        rest = jnp.concatenate([after(done[0][:sizes[0]], [outs[0]]), done[1]], axis=0)
+        outs = weight_grad_tile([near_t, far_t], width, block, [out1], segments[1:], outs)
+        rest = send_home(rest)
+        out = jnp.concatenate([rest[:sizes[0]], out1, rest[sizes[0]:]], axis=0)
         hidden = jnp.concatenate([hidden0, hidden1, hidden2, jnp.concatenate(hidden3, axis=1)], axis=0)
         return (hidden, out, outs[0], outs[1])
 

time: 359 us -> 344 us (0.958)
  waiting for transfers between devices: 109 us -> 90 us
  starting transfers between devices: 23 us -> 35.6 us
  local copies, waits for them, and re-layouts: 34.1 us -> 25.6 us
    ppermute x2 -> x3, waiting for transfers between devices: 25.7 us -> 10.9 us  [routed(): return lax.ppermute(a, ('tensor', 'dp'), route)]
    unnamed x111 -> x88, local copies, waits for them, and re-layouts: 27.3 us -> 14.8 us
    ppermute x1 -> x2, waiting for transfers between devices: 15.8 us -> 7.28 us  [send_home(): return lax.ppermute(summed, ('tensor', 'dp'), route_back)]
    ppermute x2 -> x3, starting transfers between devices: 6.39 us -> 14.5 us  [routed(): return lax.ppermute(a, ('tensor', 'dp'), route)]
    ppermute x4, waiting for transfers between devices: 21.3 us -> 26.4 us  [forward(): lax.ppermute(send[s - 1], 'dp', x_shift(s))]
    ppermute x7 -> x8, waiting for transfers between devices: 4.93 us -> 0.39 us  [swap(): return lax.ppermute(a, 'dp', core_swap)]
    ppermute x6, starting transfers between devices: 2.49 us -> 6.93 us  [z_flip(): return lax.ppermute(a, 'tensor', [(t, t ^ k) for t in range(n_tensor)])]
    ppermute x1 -> x2, starting transfers between devices: 3.04 us -> 6.76 us  [send_home(): return lax.ppermute(summed, ('tensor', 'dp'), route_back)]
  transfers between devices with their start and end apart: 26 -> 29, of which waited for: 12 -> 11; matrix products, arithmetic and copies ran while one was open for 4% -> 6% of each run, Pallas kernels for 43% -> 49%
where the time goes in v1:
time: 344 us; the launch traced here: 343 us
  Pallas kernels  168 us (49%)
  waiting for transfers between devices  90 us (26%)
  starting transfers between devices  35.6 us (10%)
  local copies, waits for them, and re-layouts  25.6 us (7%)
  between operations  14.7 us (4%)
  other arithmetic  9.54 us (3%)
    pallas_call x24, Pallas kernels, call(): pl.pallas_call(wrapped, grid=grid, in_specs=[spec for _, spec in ins] + [...  168 us
    ppermute x6, waiting for transfers between devices, z_flip(): return lax.ppermute(a, 'tensor', [(t, t ^ k) for t in range(n_tensor)])  37.8 us
    ppermute x4, waiting for transfers between devices, forward(): lax.ppermute(send[s - 1], 'dp', x_shift(s))  26.4 us
    unnamed x88, local copies, waits for them, and re-layouts  14.8 us
    ppermute x3, starting transfers between devices, routed(): return lax.ppermute(a, ('tensor', 'dp'), route)  14.5 us
    ppermute x3, waiting for transfers between devices, routed(): return lax.ppermute(a, ('tensor', 'dp'), route)  10.9 us
    ppermute x2, waiting for transfers between devices, send_home(): return lax.ppermute(summed, ('tensor', 'dp'), route_back)  7.28 us
    ppermute x6, starting transfers between devices, z_flip(): return lax.ppermute(a, 'tensor', [(t, t ^ k) for t in range(n_tensor)])  6.93 us
  transfers between devices with their start and end apart: 29, of which 11 were waited for; matrix products, arithmetic and copies ran while one was open for 6% of the time, Pallas kernels for 49%

profile of v1, /device:TPU:2, one launch (start us, length us, event | category | flops | bytes accessed | tf_op | source)
XLA Modules:
  0.0 343.3 jit_solution(8151459353165742543)
XLA Ops:
  7.8 1.0 slice.60
  8.7 4.5 %collective-permute-start = (bf16[112,1024]{1,0:T(8,128)(2,1)S(1)}, bf16[112,1024]{1,0:T(8,128)(2,1)S(1)}, u32[]{:S(2)}, u32[]{:S(2)}) collective-permute-start(bf16[112,1024]{1,0:T(8,128)(2,1)S(1)} %slice.60), channel_id=1, source_target_pairs={{0,0},{1,5},{2,8},{3,13},{4,4},{5,1},{6,12},{7,9},{8,10},{9,15},{1... | collective-permute-start | bytes 688136 | tf_op jit(solution)/shard_map/ppermute | solution.py:363
  13.2 10.9 %collective-permute-done = bf16[112,1024]{1,0:T(8,128)(2,1)S(1)} collective-permute-done((bf16[112,1024]{1,0:T(8,128)(2,1)S(1)}, bf16[112,1024]{1,0:T(8,128)(2,1)S(1)}, u32[]{:S(2)}, u32[]{:S(2)}) %collective-permute-start) | collective-permute-done | bytes 229408 | tf_op jit(solution)/shard_map/ppermute | solution.py:363
  24.2 6.0 %collective-permute-done.1 = bf16[112,1024]{1,0:T(8,128)(2,1)S(1)} collective-permute-done((bf16[112,1024]{1,0:T(8,128)(2,1)S(1)}, bf16[112,1024]{1,0:T(8,128)(2,1)S(1)}, u32[]{:S(2)}, u32[]{:S(2)}) %collective-permute-start.1) | collective-permute-done | bytes 229408 | tf_op jit(solution)/shard_map/ppermute | solution.py:304
  30.7 1.6 slice.66
  32.3 5.0 %collective-permute-start.7 = (bf16[64,1024]{1,0:T(8,128)(2,1)}, bf16[64,1024]{1,0:T(8,128)(2,1)S(1)}, u32[]{:S(2)}, u32[]{:S(2)}) collective-permute-start(bf16[64,1024]{1,0:T(8,128)(2,1)} %slice.66), channel_id=1, source_target_pairs={{0,0},{1,5},{2,8},{3,13},{4,4},{5,1},{6,12},{7,9},{8,10},{9,15},{1... | collective-permute-start | bytes 393224 | tf_op jit(solution)/shard_map/ppermute | solution.py:363
  37.2 17.8 %collective-permute-done.2.refs_2_ = bf16[2,112,1024]{2,1,0:T(8,128)(2,1)S(1)} collective-permute-done((bf16[2,112,1024]{2,1,0:T(8,128)(2,1)S(1)}, bf16[2,112,1024]{2,1,0:T(8,128)(2,1)S(1)}, u32[]{:S(2)}, u32[]{:S(2)}) %collective-permute-start.2) | collective-permute-done | bytes 458784 | tf_op jit(solution)/shard_map/ppermute | solution.py:304
  55.2 0.6 copy-done.20
  55.8 13.5 %shard_map.103 = (f32[2,32,3840]{2,1,0:T(8,128)S(1)}, bf16[1,2,32,3840]{3,2,1,0:T(8,128)(2,1)}) custom-call(bf16[64,1024]{1,0:T(8,128)(2,1)S(1)} %get-tuple-element.42.refs_0_, bf16[64,1024]{1,0:T(8,128)(2,1)S(1)} %get-tuple-element.43.refs_1_.refs_4_, bf16[1024,3840]{1,0:T(8,128)(2,1)} %refs_3_.7, ...), custom_call_target="tpu_custom_call" | custom-call | flops 2013265920 | bytes 31457280 | tf_op jit(solution)/shard_map/pallas_call | solution.py:51
  69.6 0.6 copy-done.39
  70.6 0.7 copy.13.refs_5_
  71.4 8.0 %collective-permute-done.5.refs_1_.refs_3_ = bf16[2,32,3840]{2,1,0:T(8,128)(2,1)} collective-permute-done((bf16[2,32,3840]{2,1,0:T(8,128)(2,1)}, bf16[2,32,3840]{2,1,0:T(8,128)(2,1)}, u32[]{:S(2)}, u32[]{:S(2)}) %collective-permute-start.5) | collective-permute-done | bytes 491552 | tf_op jit(solution)/shard_map/ppermute | solution.py:347
  79.4 2.9 shard_map.104
  82.3 0.7 copy-done.35
  83.0 2.2 collective-permute-start.8
  85.2 0.9 slice.70.refs_0_
  86.4 5.0 %collective-permute-start.12 = (bf16[80,1024]{1,0:T(8,128)(2,1)S(1)}, bf16[80,1024]{1,0:T(8,128)(2,1)S(1)}, u32[]{:S(2)}, u32[]{:S(2)}) collective-permute-start(bf16[80,1024]{1,0:T(8,128)(2,1)S(1)} %shard_map.111), channel_id=1, source_target_pairs={{0,0},{1,5},{2,8},{3,13},{4,4},{5,1},{6,12},{7,9},{8,10},{9,15},{1... | collective-permute-start | bytes 491528 | tf_op jit(solution)/shard_map/ppermute | solution.py:363
  91.5 2.3 collective-permute-start.9
  93.9 13.5 %shard_map.106 = (f32[2,80,3840]{2,1,0:T(8,128)S(1)}, bf16[1,2,80,3840]{3,2,1,0:T(8,128)(2,1)}) custom-call(bf16[160,1024]{1,0:T(8,128)(2,1)S(1)} %get-tuple-element.47.refs_0_.refs_1_, bf16[160,1024]{1,0:T(8,128)(2,1)S(1)} %get-tuple-element.48.refs_1_.refs_5_, bf16[1024,3840]{1,0:T(8,128)(2,1)} %refs_3_.7, ...), custom_call_target="tpu_custom_call" | custom-call | flops 5033164800 | bytes 31457280 | tf_op jit(solution)/shard_map/pallas_call | solution.py:51
  107.4 1.4 copy-done.2
  108.8 0.7 collective-permute-done.9.refs_2_
  109.9 13.2 %shard_map.109 = (f32[2,64,3840]{2,1,0:T(8,128)S(1)}, bf16[1,2,64,3840]{3,2,1,0:T(8,128)(2,1)}) custom-call(bf16[128,1024]{1,0:T(8,128)(2,1)S(1)} %get-tuple-element.52.refs_0_.refs_1_.refs_2_, bf16[128,1024]{1,0:T(8,128)(2,1)S(1)} %get-tuple-element.53.refs_1_.refs_6_, bf16[1024,3840]{1,0:T(8,128)(2,1)} %refs_3_.7, ...), custom_call_target="tpu_custom_call" | custom-call | flops 4026531840 | bytes 31457280 | tf_op jit(solution)/shard_map/pallas_call | solution.py:51
  123.1 1.3 copy-done.4
  124.4 1.3 collective-permute-start.11
  125.7 0.7 pad_maximum_fusion.6.refs_1_
  126.4 1.9 collective-permute-start.14
  128.3 1.1 fusion
  129.6 13.3 %collective-permute-done.14.refs_2_ = bf16[2,80,1024]{2,1,0:T(8,128)(2,1)} collective-permute-done((bf16[2,80,1024]{2,1,0:T(8,128)(2,1)}, bf16[2,80,1024]{2,1,0:T(8,128)(2,1)}, u32[]{:S(2)}, u32[]{:S(2)}) %collective-permute-start.14) | collective-permute-done | bytes 327712 | tf_op jit(solution)/shard_map/ppermute | solution.py:304
  142.9 1.4 shard_map.113
  144.3 1.5 copy-done.5
  145.9 1.1 copy-done.14
  146.9 4.6 %shard_map.110 = (bf16[80,3840]{1,0:T(8,128)(2,1)S(1)}, bf16[2,80,3840]{2,1,0:T(8,128)(2,1)}) custom-call(f32[2,80,3840]{2,1,0:T(8,128)S(1)} %copy-done.3, bf16[2,80,3840]{2,1,0:T(8,128)(2,1)} %collective-permute-done.6.refs_1_.refs_3_, f32[2,80,3840]{2,1,0:T(8,128)S(1)} %copy-done.3, bf16[2,80,3840]{2,1,0:T(8,128)(2,1)} %collective-permute-done.6.refs_1_.refs_3_, ...), custom_call_target="tpu_custom_call" | custom-call | flops 12288000 | bytes 6144000 | tf_op jit(solution)/shard_map/pallas_call | solution.py:51
  151.6 0.8 copy-done.28
  152.4 1.8 collective-permute-start.15
  154.3 15.9 %shard_map.114 = (bf16[2,64,3840]{2,1,0:T(8,128)(2,1)}, bf16[2,2,32,1024]{3,2,1,0:T(8,128)(2,1)}) custom-call(s32[1]{0:T(128)} %bitcast.refs_0_, bf16[2,32,3840]{2,1,0:T(8,128)(2,1)} %copy-done.11, bf16[2,32,3840]{2,1,0:T(8,128)(2,1)} %copy-done.18, bf16[1024,3840]{1,0:T(8,128)(2,1)} %refs_3_.7, bf16[1024,3840]{1,0:T(8,128)(2,1)} %refs_4_.17, ...), custom_call_target="tpu_custom_call" | custom-call | flops 2013265920 | bytes 31457280 | tf_op jit(solution)/shard_map/pallas_call | solution.py:51
  170.3 2.5 shard_map.115
  172.8 14.7 %shard_map.116 = (f32[2,80,3840]{2,1,0:T(8,128)}, bf16[1,2,80,3840]{3,2,1,0:T(8,128)(2,1)}) custom-call(bf16[160,1024]{1,0:T(8,128)(2,1)S(1)} %get-tuple-element.57.refs_3_.refs_0_, bf16[160,1024]{1,0:T(8,128)(2,1)S(1)} %get-tuple-element.58.refs_7_.refs_1_, bf16[1024,3840]{1,0:T(8,128)(2,1)} %refs_3_.7, ...), custom_call_target="tpu_custom_call" | custom-call | flops 5033164800 | bytes 31457280 | tf_op jit(solution)/shard_map/pallas_call | solution.py:51
  188.4 1.8 slice.67.refs_4_
  190.9 1.6 shard_map.119.refs_8_.refs_1_
  192.5 1.0 copy-done.7
  193.5 1.5 copy-done.6
  195.0 2.8 shard_map.117
  197.8 1.7 collective-permute-start.19
  199.5 18.3 %collective-permute-done.16.refs_1_.refs_3_ = bf16[2,80,3840]{2,1,0:T(8,128)(2,1)} collective-permute-done((bf16[2,80,3840]{2,1,0:T(8,128)(2,1)}, bf16[2,80,3840]{2,1,0:T(8,128)(2,1)}, u32[]{:S(2)}, u32[]{:S(2)}) %collective-permute-start.16) | collective-permute-done | bytes 1228832 | tf_op jit(solution)/shard_map/ppermute | solution.py:347
  217.8 4.7 %shard_map.118 = (bf16[80,3840]{1,0:T(8,128)(2,1)S(1)}, bf16[2,80,3840]{2,1,0:T(8,128)(2,1)}) custom-call(f32[2,80,3840]{2,1,0:T(8,128)S(1)} %copy-done.1, bf16[2,80,3840]{2,1,0:T(8,128)(2,1)} %collective-permute-done.16.refs_1_.refs_3_, f32[2,80,3840]{2,1,0:T(8,128)S(1)} %copy-done.1, bf16[2,80,3840]{2,1,0:T(8,128)(2,1)} %collective-permute-done.16.refs_1_.refs_3_, ...), custom_call_target="tpu_custom_call" | custom-call | flops 12288000 | bytes 6144000 | tf_op jit(solution)/shard_map/pallas_call | solution.py:51
  222.8 17.5 %shard_map.120 = (bf16[2,160,3840]{2,1,0:T(8,128)(2,1)}, bf16[2,2,80,1024]{3,2,1,0:T(8,128)(2,1)}) custom-call(s32[1]{0:T(128)} %bitcast.refs_0_, bf16[2,80,3840]{2,1,0:T(8,128)(2,1)} %get-tuple-element.59.refs_7_.refs_1_, bf16[2,80,3840]{2,1,0:T(8,128)(2,1)} %collective-permute-done.15.refs_7_.refs_2_, bf16[1024,3840]{1,0:T(8,128)(2,1)} %refs_3_.7, ...), custom_call_target="tpu_custom_call" | custom-call | flops 5033164800 | bytes 31457280 | tf_op jit(solution)/shard_map/pallas_call | solution.py:51
  240.3 2.1 pad_maximum_fusion.2
  242.6 17.3 %shard_map.121 = (bf16[2,128,3840]{2,1,0:T(8,128)(2,1)}, bf16[2,2,64,1024]{3,2,1,0:T(8,128)(2,1)}) custom-call(s32[1]{0:T(128)} %bitcast.refs_0_, bf16[2,64,3840]{2,1,0:T(8,128)(2,1)} %get-tuple-element.65.refs_6_.refs_1_, bf16[2,64,3840]{2,1,0:T(8,128)(2,1)} %collective-permute-done.19.refs_2_, bf16[1024,3840]{1,0:T(8,128)(2,1)} %refs_3_.7, ...), custom_call_target="tpu_custom_call" | custom-call | flops 4026531840 | bytes 31457280 | tf_op jit(solution)/shard_map/pallas_call | solution.py:51
  260.5 2.3 collective-permute-done.20.refs_2_.refs_6_
  262.8 17.5 %shard_map.122 = (bf16[2,160,3840]{2,1,0:T(8,128)(2,1)}, bf16[2,2,80,1024]{3,2,1,0:T(8,128)(2,1)}) custom-call(s32[1]{0:T(128)} %bitcast.refs_0_, bf16[2,80,3840]{2,1,0:T(8,128)(2,1)} %get-tuple-element.68.refs_7_.refs_1_.refs_5_, bf16[2,80,3840]{2,1,0:T(8,128)(2,1)} %collective-permute-done.20.refs_2_.refs_6_, bf16[1024,3840]{1,0:T(8,128)(2,1)} %refs_3_.7, ...), custom_call_target="tpu_custom_call" | custom-call | flops 5033164800 | bytes 31457280 | tf_op jit(solution)/shard_map/pallas_call | solution.py:51
  280.3 2.3 pad_maximum_fusion.1
  282.7 1.6 slice_bitcast_fusion
  284.3 2.1 collective-permute-start.26
  286.4 0.8 slice_bitcast_fusion.1.refs_0_
  287.3 0.9 copy-done.36
  288.2 17.0 %shard_map.123 = (bf16[1024,3840]{1,0:T(8,128)(2,1)}, bf16[1024,3840]{1,0:T(8,128)(2,1)}) custom-call(bf16[1024,512]{1,0:T(8,128)(2,1)S(1)} %copy-done.13, bf16[1024,512]{1,0:T(8,128)(2,1)S(1)} %copy-done.8, bf16[2,64,3840]{2,1,0:T(8,128)(2,1)} %get-tuple-element.60.refs_8_.refs_2_, bf16[2,160,3840]{2,1,0:T(8,128)(2,1)} %get-tuple-element.71.refs_7_.refs_3_, ...), custom_call_target="tpu_custom_call" | custom-call | flops 12884901888 | bytes 25165824 | tf_op jit(solution)/shard_map/pallas_call | solution.py:51
  305.3 3.2 copy-done
  308.5 4.8 %reduce-scatter.5.cloned.1.call-done = bf16[1,144,1024]{2,1,0:T(8,128)(2,1)} async-done(((bf16[4,144,1024]{2,1,0:T(8,128)(2,1)}), bf16[1,144,1024]{2,1,0:T(8,128)(2,1)}) %reduce-scatter.5.cloned.1.call-update) | async-done | bytes 294928 | tf_op jit(solution)/shard_map/reduce_scatter | solution.py:329
  313.3 1.0 pad_maximum_fusion.5
  314.3 4.6 %collective-permute-start.25 = (bf16[176,1024]{1,0:T(8,128)(2,1)S(1)}, bf16[176,1024]{1,0:T(8,128)(2,1)S(1)}, u32[]{:S(2)}, u32[]{:S(2)}) collective-permute-start(bf16[176,1024]{1,0:T(8,128)(2,1)S(1)} %pad_maximum_fusion.5), channel_id=1, source_target_pairs={{0,0},{5,1},{8,2},{13,3},{4,4},{1,5},{12,6},{9,7},{10,8},{15,9},{2... | collective-permute-start | bytes 1081352 | tf_op jit(solution)/shard_map/ppermute | solution.py:310
  319.0 2.5 pad_maximum_fusion
  321.5 6.8 %shard_map.125 = (bf16[1024,3840]{1,0:T(8,128)(2,1)}, bf16[1024,3840]{1,0:T(8,128)(2,1)}) custom-call(bf16[1024,512]{1,0:T(8,128)(2,1)S(1)} %copy-done.13, bf16[1024,512]{1,0:T(8,128)(2,1)S(1)} %copy-done.8, bf16[2,64,3840]{2,1,0:T(8,128)(2,1)} %get-tuple-element.60.refs_8_.refs_2_, ...), custom_call_target="tpu_custom_call", output_to_operand_aliasing={{0}: (12, {}), {1}: (13, {})} | custom-call | flops 3221225472 | bytes 6291456 | tf_op jit(solution)/shard_map/pallas_call | solution.py:51
  328.3 7.3 %collective-permute-done.25 = bf16[176,1024]{1,0:T(8,128)(2,1)S(1)} collective-permute-done((bf16[176,1024]{1,0:T(8,128)(2,1)S(1)}, bf16[176,1024]{1,0:T(8,128)(2,1)S(1)}, u32[]{:S(2)}, u32[]{:S(2)}) %collective-permute-start.25) | collective-permute-done | bytes 360480 | tf_op jit(solution)/shard_map/ppermute | solution.py:310
  335.6 0.8 pad_maximum_fusion.3
  (136 shorter events, 5.5 us)
Async XLA Ops:
  7.2 275.5 %reduce-scatter.3.cloned.1.call-start = ((), (), s32[]{:S(2)}) async-start(), calls=%async_computation.2 | async-start | bytes 1146880 | tf_op jit(solution)/shard_map/reduce_scatter | solution.py:329
  7.2 47.9 %collective-permute-start.3 = (bf16[1024,3840]{1,0:T(8,128)(2,1)}, bf16[1024,3840]{1,0:T(8,128)(2,1)}, u32[]{:S(2)}, u32[]{:S(2)}) collective-permute-start(bf16[1024,3840]{1,0:T(8,128)(2,1)} %refs_3_.7), channel_id=1, source_target_pairs={{0,1},{1,0},{2,3},{3,2},{4,5},{5,4},{6,7},{7,6},{8,9},{9,8},{10,11... | collective-permute-start | bytes 23592968 | tf_op jit(solution)/shard_map/ppermute | solution.py:307
  7.3 47.9 %collective-permute-start.4 = (bf16[1024,3840]{1,0:T(8,128)(2,1)}, bf16[1024,3840]{1,0:T(8,128)(2,1)}, u32[]{:S(2)}, u32[]{:S(2)}) collective-permute-start(bf16[1024,3840]{1,0:T(8,128)(2,1)} %refs_4_.17), channel_id=1, source_target_pairs={{0,1},{1,0},{2,3},{3,2},{4,5},{5,4},{6,7},{7,6},{8,9},{9,8},{10,11... | collective-permute-start | bytes 23592968 | tf_op jit(solution)/shard_map/ppermute | solution.py:307
  8.7 15.4 %collective-permute-start = (bf16[112,1024]{1,0:T(8,128)(2,1)S(1)}, bf16[112,1024]{1,0:T(8,128)(2,1)S(1)}, u32[]{:S(2)}, u32[]{:S(2)}) collective-permute-start(bf16[112,1024]{1,0:T(8,128)(2,1)S(1)} %slice.60), channel_id=1, source_target_pairs={{0,0},{1,5},{2,8},{3,13},{4,4},{5,1},{6,12},{7,9},{8,10},{9,15},{1... | collective-permute-start | bytes 688136 | tf_op jit(solution)/shard_map/ppermute | solution.py:363
  24.2 6.0 %collective-permute-start.1 = (bf16[112,1024]{1,0:T(8,128)(2,1)S(1)}, bf16[112,1024]{1,0:T(8,128)(2,1)S(1)}, u32[]{:S(2)}, u32[]{:S(2)}) collective-permute-start(bf16[112,1024]{1,0:T(8,128)(2,1)S(1)} %collective-permute-done), channel_id=1, source_target_pairs={{0,4},{4,0},{8,12},{12,8},{1,5},{5,1},{9,13},{13,9},{2,6},{6,2},{1... | collective-permute-start | bytes 688136 | tf_op jit(solution)/shard_map/ppermute | solution.py:304
  30.2 24.8 %collective-permute-start.2 = (bf16[2,112,1024]{2,1,0:T(8,128)(2,1)S(1)}, bf16[2,112,1024]{2,1,0:T(8,128)(2,1)S(1)}, u32[]{:S(2)}, u32[]{:S(2)}) collective-permute-start(bf16[2,112,1024]{2,1,0:T(8,128)(2,1)S(1)} %pad_maximum_fusion.4.refs_1_), channel_id=1, source_target_pairs={{0,8},{4,12},{8,0},{12,4},{1,9},{5,13},{9,1},{13,5},{2,10},{6,14},... | collective-permute-start | bytes 1376264 | tf_op jit(solution)/shard_map/ppermute | solution.py:304
  32.3 50.8 %collective-permute-start.7 = (bf16[64,1024]{1,0:T(8,128)(2,1)}, bf16[64,1024]{1,0:T(8,128)(2,1)S(1)}, u32[]{:S(2)}, u32[]{:S(2)}) collective-permute-start(bf16[64,1024]{1,0:T(8,128)(2,1)} %slice.66), channel_id=1, source_target_pairs={{0,0},{1,5},{2,8},{3,13},{4,4},{5,1},{6,12},{7,9},{8,10},{9,15},{1... | collective-permute-start | bytes 393224 | tf_op jit(solution)/shard_map/ppermute | solution.py:363
  55.1 14.1 %copy-start.30 = (bf16[64,1024]{1,0:T(8,128)(2,1)}, bf16[64,1024]{1,0:T(8,128)(2,1)S(1)}, u32[]{:S(2)}) copy-start(bf16[64,1024]{1,0:T(8,128)(2,1)S(1)} %get-tuple-element.42.refs_0_) | copy-start | bytes 393220
  55.1 14.1 %copy-start.32 = (bf16[64,1024]{1,0:T(8,128)(2,1)}, bf16[64,1024]{1,0:T(8,128)(2,1)S(1)}, u32[]{:S(2)}) copy-start(bf16[64,1024]{1,0:T(8,128)(2,1)S(1)} %get-tuple-element.43.refs_1_.refs_4_) | copy-start | bytes 393220
  55.8 13.6 %copy-start.43 = (f32[4]{0:T(128)S(1)}, f32[4]{0:T(128)}, u32[]{:S(2)}) copy-start(f32[4]{0:T(128)} %param.13) | copy-start | bytes 52
  55.8 13.7 %copy-start.41 = (s32[256]{0:T(256)S(1)}, s32[256]{0:T(256)}, u32[]{:S(2)}) copy-start(s32[256]{0:T(256)} %param.11) | copy-start | bytes 3076
  55.8 13.7 %copy-start.42 = (s32[256]{0:T(256)S(1)}, s32[256]{0:T(256)}, u32[]{:S(2)}) copy-start(s32[256]{0:T(256)} %param.12) | copy-start | bytes 3076
  55.8 23.6 %copy-start.9 = (bf16[256,3840]{1,0:T(8,128)(2,1)S(1)}, bf16[256,3840]{1,0:T(8,128)(2,1)}, u32[]{:S(2)}) copy-start(bf16[256,3840]{1,0:T(8,128)(2,1)} %refs_4_.10) | copy-start | bytes 5898244
  69.3 10.1 %collective-permute-start.5 = (bf16[2,32,3840]{2,1,0:T(8,128)(2,1)}, bf16[2,32,3840]{2,1,0:T(8,128)(2,1)}, u32[]{:S(2)}, u32[]{:S(2)}) collective-permute-start(bf16[2,32,3840]{2,1,0:T(8,128)(2,1)} %bitcast.3), channel_id=1, source_target_pairs={{0,2},{1,3},{2,0},{3,1},{4,6},{5,7},{6,4},{7,5},{8,10},{9,11},{10,... | collective-permute-start | bytes 1474568 | tf_op jit(solution)/shard_map/ppermute | solution.py:347
  79.4 6.8 %copy-start.21 = (bf16[2,112,1024]{2,1,0:T(8,128)(2,1)S(1)}, bf16[2,112,1024]{2,1,0:T(8,128)(2,1)}, u32[]{:S(2)}) copy-start(bf16[2,112,1024]{2,1,0:T(8,128)(2,1)} %copy-done.20) | copy-start | bytes 1376260
  83.0 24.3 %copy-start.11 = (bf16[2,32,3840]{2,1,0:T(8,128)(2,1)}, bf16[2,32,3840]{2,1,0:T(8,128)(2,1)S(1)}, u32[]{:S(2)}) copy-start(bf16[2,32,3840]{2,1,0:T(8,128)(2,1)S(1)} %get-tuple-element.49.refs_6_.refs_1_) | copy-start | bytes 1474564
  83.0 8.4 %collective-permute-start.8 = (bf16[64,1024]{1,0:T(8,128)(2,1)S(1)}, bf16[64,1024]{1,0:T(8,128)(2,1)S(1)}, u32[]{:S(2)}, u32[]{:S(2)}) collective-permute-start(bf16[64,1024]{1,0:T(8,128)(2,1)S(1)} %shard_map.107), channel_id=1, source_target_pairs={{0,4},{4,0},{8,12},{12,8},{1,5},{5,1},{9,13},{13,9},{2,6},{6,2},{1... | collective-permute-start | bytes 393224 | tf_op jit(solution)/shard_map/ppermute | solution.py:304
  86.3 21.0 %copy-start.22 = (bf16[160,1024]{1,0:T(8,128)(2,1)}, bf16[160,1024]{1,0:T(8,128)(2,1)S(1)}, u32[]{:S(2)}) copy-start(bf16[160,1024]{1,0:T(8,128)(2,1)S(1)} %get-tuple-element.47.refs_0_.refs_1_) | copy-start | bytes 983044
  86.4 21.0 %copy-start.24 = (bf16[160,1024]{1,0:T(8,128)(2,1)}, bf16[160,1024]{1,0:T(8,128)(2,1)S(1)}, u32[]{:S(2)}) copy-start(bf16[160,1024]{1,0:T(8,128)(2,1)S(1)} %get-tuple-element.48.refs_1_.refs_5_) | copy-start | bytes 983044
  86.4 23.4 %collective-permute-start.12 = (bf16[80,1024]{1,0:T(8,128)(2,1)S(1)}, bf16[80,1024]{1,0:T(8,128)(2,1)S(1)}, u32[]{:S(2)}, u32[]{:S(2)}) collective-permute-start(bf16[80,1024]{1,0:T(8,128)(2,1)S(1)} %shard_map.111), channel_id=1, source_target_pairs={{0,0},{1,5},{2,8},{3,13},{4,4},{5,1},{6,12},{7,9},{8,10},{9,15},{1... | collective-permute-start | bytes 491528 | tf_op jit(solution)/shard_map/ppermute | solution.py:363
  91.4 18.4 %collective-permute-start.10 = (bf16[2,32,3840]{2,1,0:T(8,128)(2,1)S(1)}, bf16[2,32,3840]{2,1,0:T(8,128)(2,1)S(1)}, u32[]{:S(2)}, u32[]{:S(2)}) collective-permute-start(bf16[2,32,3840]{2,1,0:T(8,128)(2,1)S(1)} %get-tuple-element.49.refs_6_.refs_1_), channel_id=1, source_target_pairs={{0,2},{1,3},{2,0},{3,1},{4,6},{5,7},{6,4},{7,5},{8,10},{9,11},{10,... | collective-permute-start | bytes 1474568 | tf_op jit(solution)/shard_map/ppermute | solution.py:357
  91.5 18.0 %collective-permute-start.9 = (bf16[2,64,1024]{2,1,0:T(8,128)(2,1)S(1)}, bf16[2,64,1024]{2,1,0:T(8,128)(2,1)S(1)}, u32[]{:S(2)}, u32[]{:S(2)}) collective-permute-start(bf16[2,64,1024]{2,1,0:T(8,128)(2,1)S(1)} %pad_maximum_fusion.7.refs_1_), channel_id=1, source_target_pairs={{0,8},{4,12},{8,0},{12,4},{1,9},{5,13},{9,1},{13,5},{2,10},{6,14},... | collective-permute-start | bytes 786440 | tf_op jit(solution)/shard_map/ppermute | solution.py:304
  108.8 35.5 %collective-permute-start.6 = (bf16[2,80,3840]{2,1,0:T(8,128)(2,1)}, bf16[2,80,3840]{2,1,0:T(8,128)(2,1)}, u32[]{:S(2)}, u32[]{:S(2)}) collective-permute-start(bf16[2,80,3840]{2,1,0:T(8,128)(2,1)} %bitcast.5), channel_id=1, source_target_pairs={{0,2},{1,3},{2,0},{3,1},{4,6},{5,7},{6,4},{7,5},{8,10},{9,11},{10,... | collective-permute-start | bytes 3686408 | tf_op jit(solution)/shard_map/ppermute | solution.py:347
  109.7 13.4 %copy-start.16 = (bf16[128,1024]{1,0:T(8,128)(2,1)}, bf16[128,1024]{1,0:T(8,128)(2,1)S(1)}, u32[]{:S(2)}) copy-start(bf16[128,1024]{1,0:T(8,128)(2,1)S(1)} %get-tuple-element.52.refs_0_.refs_1_.refs_2_) | copy-start | bytes 786436
  109.7 13.4 %copy-start.26 = (bf16[128,1024]{1,0:T(8,128)(2,1)}, bf16[128,1024]{1,0:T(8,128)(2,1)S(1)}, u32[]{:S(2)}) copy-start(bf16[128,1024]{1,0:T(8,128)(2,1)S(1)} %get-tuple-element.53.refs_1_.refs_6_) | copy-start | bytes 786436
  109.8 15.9 %collective-permute-start.13 = (bf16[80,1024]{1,0:T(8,128)(2,1)S(1)}, bf16[80,1024]{1,0:T(8,128)(2,1)S(1)}, u32[]{:S(2)}, u32[]{:S(2)}) collective-permute-start(bf16[80,1024]{1,0:T(8,128)(2,1)S(1)} %shard_map.112), channel_id=1, source_target_pairs={{0,4},{4,0},{8,12},{12,8},{1,5},{5,1},{9,13},{13,9},{2,6},{6,2},{1... | collective-permute-start | bytes 491528 | tf_op jit(solution)/shard_map/ppermute | solution.py:304
  109.9 13.3 %copy-start.18 = (bf16[2,32,3840]{2,1,0:T(8,128)(2,1)}, bf16[2,32,3840]{2,1,0:T(8,128)(2,1)S(1)}, u32[]{:S(2)}) copy-start(bf16[2,32,3840]{2,1,0:T(8,128)(2,1)S(1)} %collective-permute-done.10.refs_7_.refs_2_) | copy-start | bytes 1474564
  109.9 18.4 %copy-start.10 = (bf16[256,3840]{1,0:T(8,128)(2,1)S(1)}, bf16[256,3840]{1,0:T(8,128)(2,1)}, u32[]{:S(2)}) copy-start(bf16[256,3840]{1,0:T(8,128)(2,1)} %refs_4_.10) | copy-start | bytes 5898244
  124.4 5.0 %copy-start.40 = (f32[256]{0:T(256)S(1)}, f32[256]{0:T(256)}, u32[]{:S(2)}) copy-start(f32[256]{0:T(256)} %copy-done.39) | copy-start | bytes 3076
  124.4 19.9 %copy-start.3 = (f32[2,80,3840]{2,1,0:T(8,128)S(1)}, f32[2,80,3840]{2,1,0:T(8,128)}, u32[]{:S(2)}) copy-start(f32[2,80,3840]{2,1,0:T(8,128)} %copy-done.2) | copy-start | bytes 7372804
  124.4 48.4 %collective-permute-start.11 = (bf16[2,64,3840]{2,1,0:T(8,128)(2,1)}, bf16[2,64,3840]{2,1,0:T(8,128)(2,1)S(1)}, u32[]{:S(2)}, u32[]{:S(2)}) collective-permute-start(bf16[2,64,3840]{2,1,0:T(8,128)(2,1)} %bitcast.9), channel_id=1, source_target_pairs={{0,2},{1,3},{2,0},{3,1},{4,6},{5,7},{6,4},{7,5},{8,10},{9,11},{10,... | collective-permute-start | bytes 2949128 | tf_op jit(solution)/shard_map/ppermute | solution.py:347
  126.4 16.4 %collective-permute-start.14 = (bf16[2,80,1024]{2,1,0:T(8,128)(2,1)}, bf16[2,80,1024]{2,1,0:T(8,128)(2,1)}, u32[]{:S(2)}, u32[]{:S(2)}) collective-permute-start(bf16[2,80,1024]{2,1,0:T(8,128)(2,1)} %pad_maximum_fusion.6.refs_1_), channel_id=1, source_target_pairs={{0,8},{4,12},{8,0},{12,4},{1,9},{5,13},{9,1},{13,5},{2,10},{6,14},... | collective-permute-start | bytes 983048 | tf_op jit(solution)/shard_map/ppermute | solution.py:304
  144.3 1.5 copy-start.5
  152.4 17.8 %copy-start.17 = (bf16[128,1024]{1,0:T(8,128)(2,1)S(1)}, bf16[128,1024]{1,0:T(8,128)(2,1)}, u32[]{:S(2)}) copy-start(bf16[128,1024]{1,0:T(8,128)(2,1)} %copy-done.16) | copy-start | bytes 786436
  152.4 17.8 %copy-start.23 = (bf16[160,1024]{1,0:T(8,128)(2,1)S(1)}, bf16[160,1024]{1,0:T(8,128)(2,1)}, u32[]{:S(2)}) copy-start(bf16[160,1024]{1,0:T(8,128)(2,1)} %copy-done.22) | copy-start | bytes 983044
  152.4 17.8 %copy-start.25 = (bf16[160,1024]{1,0:T(8,128)(2,1)S(1)}, bf16[160,1024]{1,0:T(8,128)(2,1)}, u32[]{:S(2)}) copy-start(bf16[160,1024]{1,0:T(8,128)(2,1)} %copy-done.24) | copy-start | bytes 983044
  152.4 17.8 %copy-start.27 = (bf16[128,1024]{1,0:T(8,128)(2,1)S(1)}, bf16[128,1024]{1,0:T(8,128)(2,1)}, u32[]{:S(2)}) copy-start(bf16[128,1024]{1,0:T(8,128)(2,1)} %copy-done.26) | copy-start | bytes 786436
  152.4 17.8 %copy-start.31 = (bf16[64,1024]{1,0:T(8,128)(2,1)S(1)}, bf16[64,1024]{1,0:T(8,128)(2,1)}, u32[]{:S(2)}) copy-start(bf16[64,1024]{1,0:T(8,128)(2,1)} %copy-done.30) | copy-start | bytes 393220
  152.4 17.8 %copy-start.33 = (bf16[64,1024]{1,0:T(8,128)(2,1)S(1)}, bf16[64,1024]{1,0:T(8,128)(2,1)}, u32[]{:S(2)}) copy-start(bf16[64,1024]{1,0:T(8,128)(2,1)} %copy-done.32) | copy-start | bytes 393220
  152.4 41.0 %collective-permute-start.15 = (bf16[2,80,3840]{2,1,0:T(8,128)(2,1)}, bf16[2,80,3840]{2,1,0:T(8,128)(2,1)}, u32[]{:S(2)}, u32[]{:S(2)}) collective-permute-start(bf16[2,80,3840]{2,1,0:T(8,128)(2,1)} %get-tuple-element.59.refs_7_.refs_1_), channel_id=1, source_target_pairs={{0,2},{1,3},{2,0},{3,1},{4,6},{5,7},{6,4},{7,5},{8,10},{9,11},{10,... | collective-permute-start | bytes 3686408 | tf_op jit(solution)/shard_map/ppermute | solution.py:357
  172.8 14.7 %copy-start.12 = (bf16[1024,512]{1,0:T(8,128)(2,1)}, bf16[1024,512]{1,0:T(8,128)(2,1)S(1)}, u32[]{:S(2)}) copy-start(bf16[1024,512]{1,0:T(8,128)(2,1)S(1)} %get-tuple-element.61.refs_6_.refs_0_) | copy-start | bytes 3145732
  187.5 6.0 %copy-start.1 = (f32[2,80,3840]{2,1,0:T(8,128)S(1)}, f32[2,80,3840]{2,1,0:T(8,128)}, u32[]{:S(2)}) copy-start(f32[2,80,3840]{2,1,0:T(8,128)} %get-tuple-element.62.refs_6_.refs_0_.refs_2_) | copy-start | bytes 7372804
  187.5 30.3 %collective-permute-start.16 = (bf16[2,80,3840]{2,1,0:T(8,128)(2,1)}, bf16[2,80,3840]{2,1,0:T(8,128)(2,1)}, u32[]{:S(2)}, u32[]{:S(2)}) collective-permute-start(bf16[2,80,3840]{2,1,0:T(8,128)(2,1)} %bitcast.13), channel_id=1, source_target_pairs={{0,2},{1,3},{2,0},{3,1},{4,6},{5,7},{6,4},{7,5},{8,10},{9,11},{10,... | collective-permute-start | bytes 3686408 | tf_op jit(solution)/shard_map/ppermute | solution.py:347
  187.9 3.0 collective-permute-start.17
  187.9 34.9 %collective-permute-start.18 = (bf16[2,64,3840]{2,1,0:T(8,128)(2,1)}, bf16[2,64,3840]{2,1,0:T(8,128)(2,1)}, u32[]{:S(2)}, u32[]{:S(2)}) collective-permute-start(bf16[2,64,3840]{2,1,0:T(8,128)(2,1)} %get-tuple-element.60.refs_8_.refs_2_), channel_id=1, source_target_pairs={{0,1},{1,0},{2,3},{3,2},{4,5},{5,4},{6,7},{7,6},{8,9},{9,8},{10,11... | collective-permute-start | bytes 2949128 | tf_op jit(solution)/shard_map/ppermute | solution.py:307
  190.5 3.0 copy-start.19
  193.5 1.5 copy-start.6
  195.0 22.8 %copy-start.15 = (bf16[80,3840]{1,0:T(8,128)(2,1)S(1)}, bf16[80,3840]{1,0:T(8,128)(2,1)}, u32[]{:S(2)}) copy-start(bf16[80,3840]{1,0:T(8,128)(2,1)} %get-tuple-element.80.refs_4_) | copy-start | bytes 1843204
  197.8 24.7 %copy-start.34 = (bf16[64,3840]{1,0:T(8,128)(2,1)}, bf16[64,3840]{1,0:T(8,128)(2,1)S(1)}, u32[]{:S(2)}) copy-start(bf16[64,3840]{1,0:T(8,128)(2,1)S(1)} %get-tuple-element.63) | copy-start | bytes 1474564
  197.8 44.7 %collective-permute-start.19 = (bf16[2,64,3840]{2,1,0:T(8,128)(2,1)}, bf16[2,64,3840]{2,1,0:T(8,128)(2,1)}, u32[]{:S(2)}, u32[]{:S(2)}) collective-permute-start(bf16[2,64,3840]{2,1,0:T(8,128)(2,1)} %get-tuple-element.65.refs_6_.refs_1_), channel_id=1, source_target_pairs={{0,2},{1,3},{2,0},{3,1},{4,6},{5,7},{6,4},{7,5},{8,10},{9,11},{10,... | collective-permute-start | bytes 2949128 | tf_op jit(solution)/shard_map/ppermute | solution.py:357
  222.5 17.8 %copy-start.38 = (bf16[2,2,32,1024]{3,2,1,0:T(8,128)(2,1)S(1)}, bf16[2,2,32,1024]{3,2,1,0:T(8,128)(2,1)}, u32[]{:S(2)}) copy-start(bf16[2,2,32,1024]{3,2,1,0:T(8,128)(2,1)} %get-tuple-element.67) | copy-start | bytes 786436
  222.5 40.3 %collective-permute-start.20 = (bf16[2,80,3840]{2,1,0:T(8,128)(2,1)}, bf16[2,80,3840]{2,1,0:T(8,128)(2,1)}, u32[]{:S(2)}, u32[]{:S(2)}) collective-permute-start(bf16[2,80,3840]{2,1,0:T(8,128)(2,1)} %get-tuple-element.68.refs_7_.refs_1_.refs_5_), channel_id=1, source_target_pairs={{0,2},{1,3},{2,0},{3,1},{4,6},{5,7},{6,4},{7,5},{8,10},{9,11},{10,... | collective-permute-start | bytes 3686408 | tf_op jit(solution)/shard_map/ppermute | solution.py:357
  242.4 70.9 %reduce-scatter.5.cloned.1.call-start = ((), (), s32[]{:S(2)}) async-start(), calls=%async_computation.3 | async-start | bytes 1474560 | tf_op jit(solution)/shard_map/reduce_scatter | solution.py:329
  242.5 44.8 %collective-permute-start.21 = (bf16[2,160,3840]{2,1,0:T(8,128)(2,1)}, bf16[2,160,3840]{2,1,0:T(8,128)(2,1)}, u32[]{:S(2)}, u32[]{:S(2)}) collective-permute-start(bf16[2,160,3840]{2,1,0:T(8,128)(2,1)} %get-tuple-element.71.refs_7_.refs_3_), channel_id=1, source_target_pairs={{0,1},{1,0},{2,3},{3,2},{4,5},{5,4},{6,7},{7,6},{8,9},{9,8},{10,11... | collective-permute-start | bytes 7372808 | tf_op jit(solution)/shard_map/ppermute | solution.py:307
  259.9 20.4 %copy-start.37 = (bf16[2,2,64,1024]{3,2,1,0:T(8,128)(2,1)S(1)}, bf16[2,2,64,1024]{3,2,1,0:T(8,128)(2,1)}, u32[]{:S(2)}) copy-start(bf16[2,2,64,1024]{3,2,1,0:T(8,128)(2,1)} %get-tuple-element.75) | copy-start | bytes 1572868
  259.9 27.4 %collective-permute-start.22 = (bf16[2,128,3840]{2,1,0:T(8,128)(2,1)}, bf16[2,128,3840]{2,1,0:T(8,128)(2,1)}, u32[]{:S(2)}, u32[]{:S(2)}) collective-permute-start(bf16[2,128,3840]{2,1,0:T(8,128)(2,1)} %get-tuple-element.72.refs_7_.refs_4_), channel_id=1, source_target_pairs={{0,1},{1,0},{2,3},{3,2},{4,5},{5,4},{6,7},{7,6},{8,9},{9,8},{10,11... | collective-permute-start | bytes 5898248 | tf_op jit(solution)/shard_map/ppermute | solution.py:307
  260.2 27.1 %collective-permute-start.23 = (bf16[2,80,3840]{2,1,0:T(8,128)(2,1)}, bf16[2,80,3840]{2,1,0:T(8,128)(2,1)}, u32[]{:S(2)}, u32[]{:S(2)}) collective-permute-start(bf16[2,80,3840]{2,1,0:T(8,128)(2,1)} %get-tuple-element.68.refs_7_.refs_1_.refs_5_), channel_id=1, source_target_pairs={{0,1},{1,0},{2,3},{3,2},{4,5},{5,4},{6,7},{7,6},{8,9},{9,8},{10,11... | collective-permute-start | bytes 3686408 | tf_op jit(solution)/shard_map/ppermute | solution.py:307
  262.8 24.5 %collective-permute-start.24 = (bf16[2,80,3840]{2,1,0:T(8,128)(2,1)}, bf16[2,80,3840]{2,1,0:T(8,128)(2,1)}, u32[]{:S(2)}, u32[]{:S(2)}) collective-permute-start(bf16[2,80,3840]{2,1,0:T(8,128)(2,1)} %collective-permute-done.20.refs_2_.refs_6_), channel_id=1, source_target_pairs={{0,1},{1,0},{2,3},{3,2},{4,5},{5,4},{6,7},{7,6},{8,9},{9,8},{10,11... | collective-permute-start | bytes 3686408 | tf_op jit(solution)/shard_map/ppermute | solution.py:307
  280.3 7.0 %copy-start.8 = (bf16[1024,512]{1,0:T(8,128)(2,1)S(1)}, bf16[1024,512]{1,0:T(8,128)(2,1)}, u32[]{:S(2)}) copy-start(bf16[1024,512]{1,0:T(8,128)(2,1)} %copy-done.7) | copy-start | bytes 3145732
  280.3 7.0 %copy-start.13 = (bf16[1024,512]{1,0:T(8,128)(2,1)S(1)}, bf16[1024,512]{1,0:T(8,128)(2,1)}, u32[]{:S(2)}) copy-start(bf16[1024,512]{1,0:T(8,128)(2,1)} %copy-done.12) | copy-start | bytes 3145732
  284.3 37.2 %collective-permute-start.26 = (bf16[80,1024]{1,0:T(8,128)(2,1)}, bf16[80,1024]{1,0:T(8,128)(2,1)S(1)}, u32[]{:S(2)}, u32[]{:S(2)}) collective-permute-start(bf16[80,1024]{1,0:T(8,128)(2,1)} %slice_bitcast_fusion), channel_id=1, source_target_pairs={{0,0},{5,1},{8,2},{13,3},{4,4},{1,5},{12,6},{9,7},{10,8},{15,9},{2... | collective-permute-start | bytes 491528 | tf_op jit(solution)/shard_map/ppermute | solution.py:310
  305.3 3.2 copy-start
  308.5 10.5 %copy-start.29 = (bf16[80,3840]{1,0:T(8,128)(2,1)S(1)}, bf16[80,3840]{1,0:T(8,128)(2,1)}, u32[]{:S(2)}) copy-start(bf16[80,3840]{1,0:T(8,128)(2,1)} %copy-done.28) | copy-start | bytes 1843204
  314.3 21.3 %collective-permute-start.25 = (bf16[176,1024]{1,0:T(8,128)(2,1)S(1)}, bf16[176,1024]{1,0:T(8,128)(2,1)S(1)}, u32[]{:S(2)}, u32[]{:S(2)}) collective-permute-start(bf16[176,1024]{1,0:T(8,128)(2,1)S(1)} %pad_maximum_fusion.5), channel_id=1, source_target_pairs={{0,0},{5,1},{8,2},{13,3},{4,4},{1,5},{12,6},{9,7},{10,8},{15,9},{2... | collective-permute-start | bytes 1081352 | tf_op jit(solution)/shard_map/ppermute | solution.py:310
  (9 other events, 8.6 us)
Sparse Core Ops, SparseCore 0:
  242.5 24.9 reduce-scatter.2
  282.8 30.5 reduce-scatter.4
